TPU v7x, 128 devices: a whole 4x4x4 slice. The times are simulated.
128 devices in a mesh: wide: 16 (over x, y), narrow: 8 (over z, core).
Axes of the slice: x: 4, y: 4, z: 4, core: 2. Of those that a mesh axis runs over, the one named last changes fastest.
Arguments:
- loads: bfloat16 [256, 524288], P('narrow', 'wide'), may hold values from -6 to 6
- state: bfloat16 [256, 524288], P('narrow', 'wide'), may hold values from -6 to 6
- modal_diag: float32 [524288], P('wide'), may hold values from 0.5 to 2
- phi: bfloat16 [4096, 128, 128], P('wide'), may hold values from -0.25 to 0.25
- incidence: int32 [4096], P('wide'), may hold values from 0 to 127
- sizes: int32 [2048], P('wide'), may hold values from 1 to 129, as said below
- factor: float32 [16384, 16384], P('wide', 'narrow'), may hold values from -0.046875 to 0.046875
Outputs:
- adjoint: bfloat16 [256, 524288], P('narrow', 'wide')
- sensitivity: float32 [256, 2048], P('narrow', 'wide')
Inputs may be any that keep to these rules, and one draw needn't show every extreme that they name: `sizes`: the 128 substructures of each group hold at most 256 tiles together, and in every draw some group holds exactly 256.
All inputs are finite; a program needn't handle non-finite values.
Results may differ from a plain program's by a relative error of at most 0.015.
Values may be sent and summed in bfloat16 or wider, within the bound.
No kernel may reach another device: no remote copies, remote signals or barrier semaphores. Data moves between devices by JAX's collectives and lax.ppermute only.
A program may use at most 128 MiB of HBM per device.

v0:
```python
import jax
import jax.numpy as jnp
from jax import lax
from jax.sharding import PartitionSpec as P

sens_scale = 0.0625


def in_blocks(shard, dim, peers):
    shape = shard.shape
    parts = shard.reshape(*shape[:dim], peers, shape[dim] // peers, *shape[dim + 1 :])
    return jnp.moveaxis(parts, dim, 0)


def summed_on_arrival(shard, axis, dim):
    peers = lax.axis_size(axis)
    parts = lax.all_to_all(in_blocks(shard, dim, peers), axis, 0, 0, tiled=True)
    return jnp.sum(parts, axis=0)


def from_everyone(shard, axis):
    peers = lax.axis_size(axis)
    return lax.all_to_all(
        jnp.broadcast_to(shard[None], (peers, *shard.shape)), axis, 0, 0, tiled=True
    )


def in_order(parts, dim):
    shape = list(parts.shape[1:])
    shape[dim] *= parts.shape[0]
    return jnp.moveaxis(parts, 0, dim).reshape(shape)


def gather_directly(shard, axis, dim):
    parts = from_everyone(shard, axis)
    return in_order(parts, dim)


def sent_and_summed(shard, axis, dim):
    peers = lax.axis_size(axis)
    parts = lax.all_to_all(in_blocks(shard, dim, peers), axis, 0, 0, tiled=True)
    return jnp.sum(parts.astype(jnp.float32), axis=0)


def body(loads, state, modal_diag, phi, incidence, sizes, factor):
    load_cols = loads.shape[0]
    tile_count = phi.shape[0]
    block_rows = phi.shape[1]
    subs_local = sizes.shape[0]
    own_rows = factor.shape[0]
    modes_all = own_rows * lax.axis_size("wide")
    block_count = modes_all // block_rows
    load_tiles = loads.reshape(load_cols, tile_count, block_rows)
    state_tiles = state.reshape(load_cols, tile_count, block_rows)
    diag_tiles = modal_diag.reshape(tile_count, block_rows)
    slot_index = jnp.arange(tile_count, dtype=jnp.int32)
    running = jnp.cumsum(sizes)
    owner_sub = jnp.sum((running[None, :] <= slot_index[:, None]).astype(jnp.int32), axis=1)
    live_slot = slot_index < running[-1]
    member = (
        (owner_sub[:, None] == jnp.arange(subs_local, dtype=jnp.int32)[None, :])
        & live_slot[:, None]
    ).astype(jnp.float32)
    chooser = (
        (incidence[:, None] == jnp.arange(block_count, dtype=jnp.int32)[None, :])
        & live_slot[:, None]
    ).astype(jnp.float32)
    tile_terms = jnp.einsum("lti,tim->ltm", load_tiles, phi, preferred_element_type=jnp.float32)
    partial_value = jnp.einsum("tn,ltm->lnm", chooser, tile_terms, precision=lax.Precision.HIGHEST)
    partial_value = partial_value.reshape(load_cols, modes_all)
    own_loads = summed_on_arrival(partial_value, "wide", 1)
    whole_loads = gather_directly(own_loads, "narrow", 0)
    image_part = sent_and_summed(
        jnp.dot(whole_loads, factor, precision=lax.Precision.HIGHEST).astype(jnp.bfloat16),
        "wide",
        0,
    )
    image = gather_directly(image_part, "wide", 0)
    own_amplitude = sent_and_summed(
        lax.dot_general(
            image, factor, (((1,), (1,)), ((), ())), precision=lax.Precision.HIGHEST
        ).astype(jnp.bfloat16),
        "narrow",
        0,
    )
    amp_round = own_amplitude.astype(jnp.bfloat16)
    amp_all = gather_directly(amp_round, "wide", 1)
    picked = jnp.take(amp_all.reshape(load_cols, block_count, block_rows), incidence, axis=1)
    coupling = jnp.einsum("ltm,tim->lti", picked, phi, preferred_element_type=jnp.float32)
    response = diag_tiles[None, :, :] * load_tiles.astype(jnp.float32) + coupling
    response = jnp.where(live_slot[None, :, None], response, jnp.zeros_like(response))
    row_totals = jnp.sum(response * state_tiles.astype(jnp.float32), axis=2) * sens_scale
    sensitivity = jnp.dot(row_totals, member, precision=lax.Precision.HIGHEST)
    adjoint = response.astype(jnp.bfloat16).reshape(load_cols, tile_count * block_rows)
    return (adjoint, sensitivity)


def solution(mesh):
    return jax.shard_map(
        body,
        mesh=mesh,
        in_specs=(
            P("narrow", "wide"),
            P("narrow", "wide"),
            P("wide"),
            P("wide", None, None),
            P("wide"),
            P("wide"),
            P("wide", "narrow"),
        ),
        out_specs=(P("narrow", "wide"), P("narrow", "wide")),
        check_vma=False,
    )
```

profile of v0, /device:TPU:0, one launch (start us, length us, event | category | flops | bytes accessed | tf_op | source)
XLA Modules:
  0.0 203.2 jit_solution(16241288599339179534)
XLA Ops:
  0.6 0.0 copy-start
  0.6 0.9 copy.26
  1.6 0.2 reduce-window.4
  1.7 0.5 slice.7
  2.2 0.6 iota_compare_fusion.3
  2.9 0.0 copy-done
  2.9 0.0 copy-start.2
  2.9 4.7 %convolution_bitcast_fusion = f32[32,256,128]{2,0,1:T(8,128)S(1)} fusion(bf16[256,128,128]{2,1,0:T(8,128)(2,1)} %param.10, bf16[32,32768]{1,0:T(8,128)(2,1)S(1)} %copy-done), kind=kOutput, calls=%fused_computation.10 | convolution fusion | flops 268435456 | bytes 14680064 | tf_op jit(solution)/shard_map/lti,tim->ltm/dot_general | solution.py:68
  7.6 0.0 copy-done.2
  7.6 6.6 %fusion.11 = f32[32,128,128]{1,2,0:T(8,128)} fusion(f32[32,256,128]{2,0,1:T(8,128)S(1)} %convolution_bitcast_fusion, s32[256]{0:T(256)S(1)} %copy-done.2, pred[256]{0:T(512)(128)(4,1)S(1)} %iota_compare_fusion.3), kind=kOutput, calls=%fused_computation.19 | convolution fusion | flops 1610678272 | bytes 6292736 | tf_op jit(solution)/shard_map/tn,ltm->lnm/dot_general | solution.py:69
  14.2 2.9 %copy.30 = f32[32,128,128]{2,1,0:T(8,128)} copy(f32[32,128,128]{1,2,0:T(8,128)} %fusion.11) | data formatting | bytes 4194304 | tf_op jit(solution)/shard_map/tn,ltm->lnm/transpose | solution.py:69
  17.2 2.7 %reshape_reshape.6 = f32[32,16,1024]{2,1,0:T(8,128)} reshape(f32[32,128,128]{2,1,0:T(8,128)} %copy.30) | data formatting | bytes 4194304 | tf_op jit(solution)/shard_map/reshape;reshape | solution.py:11
  19.9 2.8 %copy.31 = f32[16,32,1024]{2,1,0:T(8,128)S(1)} copy(f32[16,32,1024]{2,0,1:T(8,128)} %bitcast.62) | data formatting | bytes 4194304 | tf_op jit(solution)/shard_map/transpose | solution.py:12
  22.7 35.3 %all_to_all.30 = f32[16,32,1024]{2,1,0:T(8,128)} all-to-all(f32[16,32,1024]{2,1,0:T(8,128)S(1)} %copy.31), channel_id=1, replica_groups=mesh['wide'=16,'narrow'=8] {'wide'}, dimensions={0} | all-to-all | bytes 4194304 | tf_op jit(solution)/shard_map/all_to_all | solution.py:17
  58.0 1.7 reduce_sum.48
  59.7 0.1 broadcast_in_dim.27
  59.8 0.0 slice-start
  59.8 21.5 %all_to_all.31 = f32[8,32,1024]{2,1,0:T(8,128)S(1)} all-to-all(f32[8,32,1024]{2,1,0:T(8,128)S(1)} %broadcast_in_dim.27), channel_id=1, replica_groups=mesh['wide'=16,'narrow'=8] {'narrow'}, dimensions={0} | all-to-all | bytes 2097152 | tf_op jit(solution)/shard_map/all_to_all | solution.py:23
  81.3 0.0 slice-start.1
  81.3 9.7 %convolution_convert_fusion = bf16[256,2048]{1,0:T(8,128)(2,1)S(1)} fusion(f32[256,1024]{1,0:T(8,128)S(1)} %bitcast.64, f32[1024,2048]{1,0:T(8,128)} %param.13), kind=kOutput, calls=%fused_computation.8 | convolution fusion | flops 6442975232 | bytes 10485760 | tf_op jit(solution)/shard_map/dot_general | solution.py:74
  91.0 20.4 %all_to_all.32 = bf16[16,16,2048]{2,1,0:T(8,128)(2,1)S(1)} all-to-all(bf16[16,16,2048]{2,1,0:T(8,128)(2,1)S(1)} %bitcast.65), channel_id=1, replica_groups=mesh['wide'=16,'narrow'=8] {'wide'}, dimensions={0} | all-to-all | bytes 2097152 | tf_op jit(solution)/shard_map/all_to_all | solution.py:41
  111.4 0.1 convert_reduce_fusion
  111.6 0.2 broadcast_in_dim.28
  111.8 30.1 %all_to_all.33 = f32[16,16,2048]{2,1,0:T(8,128)S(1)} all-to-all(f32[16,16,2048]{2,1,0:T(8,128)S(1)} %broadcast_in_dim.28), channel_id=1, replica_groups=mesh['wide'=16,'narrow'=8] {'wide'}, dimensions={0} | all-to-all | bytes 4194304 | tf_op jit(solution)/shard_map/all_to_all | solution.py:23
  141.9 0.0 slice-done
  141.9 0.0 slice-done.1
  141.9 7.2 %convolution_convert_fusion.1 = bf16[256,1024]{1,0:T(8,128)(2,1)S(1)} fusion(f32[256,2048]{1,0:T(8,128)S(1)} %bitcast.63, f32[1024,2048]{1,0:T(8,128)S(1)} %bitcast.61), kind=kOutput, calls=%fused_computation.21 | convolution fusion | flops 6442713088 | bytes 11010048 | tf_op jit(solution)/shard_map/dot_general | solution.py:80
  149.1 12.9 %all_to_all.34 = bf16[8,32,1024]{2,1,0:T(8,128)(2,1)S(1)} all-to-all(bf16[8,32,1024]{2,1,0:T(8,128)(2,1)S(1)} %bitcast.68), channel_id=1, replica_groups=mesh['wide'=16,'narrow'=8] {'narrow'}, dimensions={0} | all-to-all | bytes 1048576 | tf_op jit(solution)/shard_map/all_to_all | solution.py:41
  162.0 0.1 reduce_sum.50
  162.0 1.1 broadcast_in_dim.29
  163.1 3.9 %all-to-all-start.5 = ((bf16[16,32,1024]{2,1,0:T(8,128)(2,1)}), bf16[16,32,1024]{2,1,0:T(8,128)(2,1)S(1)}, u32[]{:S(2)}, u32[]{:S(2)}) async-start(bf16[16,32,1024]{2,1,0:T(8,128)(2,1)} %broadcast_in_dim.29), calls=%async_computation.5 | async-start | bytes 2097152 | tf_op jit(solution)/shard_map/all_to_all | solution.py:23
  167.0 0.1 reduce.1
  167.2 0.1 convert_reduce_fusion.1
  167.3 17.0 %all-to-all-done.5 = bf16[16,32,1024]{2,1,0:T(8,128)(2,1)S(1)} async-done(((bf16[16,32,1024]{2,1,0:T(8,128)(2,1)}), bf16[16,32,1024]{2,1,0:T(8,128)(2,1)S(1)}, u32[]{:S(2)}, u32[]{:S(2)}) %all-to-all-start.5) | async-done | bytes 1048608 | tf_op jit(solution)/shard_map/all_to_all | solution.py:23
  184.3 1.5 copy.32
  185.9 2.3 %reshape_reshape.7 = bf16[32,128,128]{2,1,0:T(8,128)(2,1)} reshape(bf16[32,16,1024]{2,1,0:T(8,128)(2,1)} %copy.32) | data formatting | bytes 2097152 | tf_op jit(solution)/shard_map/reshape;reshape | solution.py:88
  188.2 1.9 copy.33
  190.1 0.0 copy-start.1
  190.1 2.2 %gather_fusion = bf16[256,32,128]{2,1,0:T(8,128)(2,1)} fusion(bf16[32,128,128]{2,0,1:T(8,128)(2,1)S(1)} %copy.33, s32[1024]{0:T(1024)S(1)} %pad_clamp_fusion), kind=kCustom, calls=%fused_computation | custom fusion | bytes 4195328 | tf_op jit(solution)/shard_map/jit(_take)/gather | solution.py:88
  192.3 0.0 copy-done.1
  192.3 8.3 %fusion = (f32[32,256]{0,1:T(8,128)S(1)}, bf16[256,4,8,128]{3,2,1,0:T(8,128)(2,1)S(1)}) fusion(f32[256,128]{1,0:T(8,128)S(1)} %bitcast.69, pred[256]{0:T(512)(128)(4,1)S(1)} %iota_compare_fusion.3, bf16[256,128,128]{2,1,0:T(8,128)(2,1)} %param.10, bf16[256,32,128]{2,1,0:T(8,128)(2,1)} %gather_fusion, pred[256]{0:T(512)(128)(4,1)S(1)} %compare_and_fusion, ...), kind=kOutput, calls=%fused_computation.2 | convolution fusion | flops 277864448 | bytes 16941568 | tf_op jit(solution)/shard_map/ltm,tim->lti/dot_general | solution.py:89
  200.6 1.7 copy.51
  202.3 0.9 fusion.16
  (4 shorter events, 0.0 us)
Async XLA Ops:
  0.6 2.3 %copy-start = (bf16[32,32768]{1,0:T(8,128)(2,1)S(1)}, bf16[32,32768]{1,0:T(8,128)(2,1)}, u32[]{:S(2)}) copy-start(bf16[32,32768]{1,0:T(8,128)(2,1)} %param.7) | copy-start | bytes 6291460
  2.9 4.7 %copy-start.2 = (s32[256]{0:T(256)S(1)}, s32[256]{0:T(256)}, u32[]{:S(2)}) copy-start(s32[256]{0:T(256)} %param.11) | copy-start | bytes 3076
  59.8 82.1 %slice-start = ((s8[8388608]{0:T(1024)(128)(4,1)}), s8[4194304]{0:T(1024)(128)(4,1)S(1)}, s32[]{:S(2)}) async-start(s8[8388608]{0:T(1024)(128)(4,1)} %bitcast.60), calls=%async_computation.6 | async-start | bytes 8388608
  81.3 60.6 %slice-start.1 = ((s8[8388608]{0:T(1024)(128)(4,1)}), s8[4194304]{0:T(1024)(128)(4,1)S(1)}, s32[]{:S(2)}) async-start(s8[8388608]{0:T(1024)(128)(4,1)} %bitcast.60), calls=%async_computation.7 | async-start | bytes 8388608
  163.1 21.2 %all-to-all-start.5 = ((bf16[16,32,1024]{2,1,0:T(8,128)(2,1)}), bf16[16,32,1024]{2,1,0:T(8,128)(2,1)S(1)}, u32[]{:S(2)}, u32[]{:S(2)}) async-start(bf16[16,32,1024]{2,1,0:T(8,128)(2,1)} %broadcast_in_dim.29), calls=%async_computation.5 | async-start | bytes 2097152 | tf_op jit(solution)/shard_map/all_to_all | solution.py:23
  190.1 2.2 %copy-start.1 = (f32[32768]{0:T(1024)S(1)}, f32[32768]{0:T(1024)}, u32[]{:S(2)}) copy-start(f32[32768]{0:T(1024)} %param.9) | copy-start | bytes 393220
where the time goes:
time: 204 us; the launch traced here: 203 us
  blocking collectives  120 us (59%)
  matrix products  37.5 us (18%)
  local copies, waits for them, and re-layouts  21 us (10%)
  waiting for transfers between devices  17 us (8%)
  starting transfers between devices  3.88 us (2%)
  other arithmetic  3 us (1%)
    all_to_all x2, blocking collectives, from_everyone(): lax.all_to_all(jnp.broadcast_to(shard[None], (peers, *shard.shape)), axis...  51.5 us
    all_to_all x1, blocking collectives, summed_on_arrival(): parts = lax.all_to_all(in_blocks(shard, dim, peers), axis, 0, 0, tiled=True)  35.3 us
    all_to_all x2, blocking collectives, sent_and_summed(): parts = lax.all_to_all(in_blocks(shard, dim, peers), axis, 0, 0, tiled=True)  33.3 us
    all_to_all x1, waiting for transfers between devices, from_everyone(): lax.all_to_all(jnp.broadcast_to(shard[None], (peers, *shard.shape)), axis...  17 us
    dot_general x1, matrix products, body(): jnp.dot(whole_loads, factor, precision=lax.Precision.HIGHEST)  9.73 us
    dot_general x1, matrix products, body(): jnp.einsum('ltm,tim->lti', picked, phi, preferred_element_type=jnp.float32)  8.31 us
    dot_general x1, matrix products, body(): lax.dot_general(image, factor, (((1,), (1,)), ((), ())), precision=lax.Pr...  7.22 us
    dot_general x1, matrix products, body(): jnp.einsum('tn,ltm->lnm', chooser, tile_terms, precision=lax.Precision.HI...  6.62 us
  transfers between devices with their start and end apart: 1, of which 1 were waited for; matrix products, arithmetic and copies ran while one was open for 0% of the time, Pallas kernels for 0%

commit v1 on v0

v1 whole, which is shorter than its diff:
```python
import jax
import jax.numpy as jnp
from jax import lax
from jax.experimental import pallas as pl
from jax.experimental.pallas import tpu as pltpu
from jax.sharding import Mesh, PartitionSpec as P

sens_scale = 0.0625
BLOCK = 128
WIDE = ("x", "y")
F32, BF16 = jnp.float32, jnp.bfloat16


def condense(inc, sizes, loads, phi, factor, peers, steps):
    load_cols = loads.shape[0]
    tiles = phi.shape[0]
    subs = sizes.shape[0]
    frows, fcols = factor.shape
    blocks = peers * frows // BLOCK
    per_step = tiles // steps

    def kernel(inc_ref, sizes_ref, loads_ref, phi_ref, f_ref, out_ref, fb_ref, acc_ref, live_ref):
        step = pl.program_id(0)

        @pl.when(step == 0)
        def _():
            acc_ref[...] = jnp.zeros_like(acc_ref)
            live_ref[0] = lax.fori_loop(0, subs, lambda s, n: n + sizes_ref[s], jnp.int32(0))

        live = live_ref[0]
        for j in range(per_step):
            tile = step * per_step + j
            term = jnp.dot(loads_ref[:, j * BLOCK : (j + 1) * BLOCK], phi_ref[j], preferred_element_type=F32)
            term = jnp.where(tile < live, term, jnp.zeros_like(term))
            acc_ref[inc_ref[tile]] += term
        fb_ref[...] = f_ref[...].astype(BF16)

        @pl.when(step == steps - 1)
        def _():
            per = blocks // peers
            for b in range(blocks):
                out_ref[b // per, :, (b % per) * BLOCK : (b % per + 1) * BLOCK] = acc_ref[b].astype(BF16)

    return pl.pallas_call(
        kernel,
        out_shape=(
            jax.ShapeDtypeStruct((peers, load_cols, frows), BF16),
            jax.ShapeDtypeStruct((frows, fcols), BF16),
        ),
        grid_spec=pltpu.PrefetchScalarGridSpec(
            num_scalar_prefetch=2,
            grid=(steps,),
            in_specs=[
                pl.BlockSpec((load_cols, per_step * BLOCK), lambda i, *_: (0, i)),
                pl.BlockSpec((per_step, BLOCK, BLOCK), lambda i, *_: (i, 0, 0)),
                pl.BlockSpec((frows // steps, fcols), lambda i, *_: (i, 0)),
            ],
            out_specs=(
                pl.BlockSpec((peers, load_cols, frows), lambda i, *_: (0, 0, 0)),
                pl.BlockSpec((frows // steps, fcols), lambda i, *_: (i, 0)),
            ),
            scratch_shapes=[
                pltpu.VMEM((blocks, load_cols, BLOCK), F32),
                pltpu.SMEM((1,), jnp.int32),
            ],
        ),
        compiler_params=pltpu.CompilerParams(vmem_limit_bytes=40 << 20),
        name="condense",
    )(inc, sizes, loads, phi, factor)


def times_factor(left, own, other, steps):
    rows, depth = left.shape
    cols = own.shape[1]
    width = cols // steps

    def kernel(left_ref, own_ref, other_ref, out_ref):
        step = pl.program_id(0)

        @pl.when(step < steps)
        def _():
            out_ref[...] = jnp.dot(left_ref[...], own_ref[...], preferred_element_type=F32).astype(BF16)

        @pl.when(step >= steps)
        def _():
            out_ref[...] = jnp.dot(left_ref[...], other_ref[...], preferred_element_type=F32).astype(BF16)

    return pl.pallas_call(
        kernel,
        out_shape=jax.ShapeDtypeStruct((rows, 2 * cols), BF16),
        grid=(2 * steps,),
        in_specs=[
            pl.BlockSpec((rows, depth), lambda i: (0, 0)),
            pl.BlockSpec((depth, width), lambda i: (0, jnp.minimum(i, steps - 1))),
            pl.BlockSpec((depth, width), lambda i: (0, jnp.maximum(i - steps, 0))),
        ],
        out_specs=pl.BlockSpec((rows, width), lambda i: (0, i)),
        compiler_params=pltpu.CompilerParams(vmem_limit_bytes=40 << 20),
        name="times_factor",
    )(left, own, other)


def times_transpose(image, own, other, steps):
    rows = image.shape[0]
    frows, cols = own.shape
    height = frows // steps
    contract = (((1,), (1,)), ((), ()))

    def kernel(image_ref, own_ref, other_ref, out_ref):
        total = lax.dot_general(image_ref[:, :cols], own_ref[...], contract, preferred_element_type=F32)
        total += lax.dot_general(image_ref[:, cols:], other_ref[...], contract, preferred_element_type=F32)
        out_ref[...] = total.astype(BF16)

    return pl.pallas_call(
        kernel,
        out_shape=jax.ShapeDtypeStruct((rows, frows), BF16),
        grid=(steps,),
        in_specs=[
            pl.BlockSpec((rows, 2 * cols), lambda i: (0, 0)),
            pl.BlockSpec((height, cols), lambda i: (i, 0)),
            pl.BlockSpec((height, cols), lambda i: (i, 0)),
        ],
        out_specs=pl.BlockSpec((rows, height), lambda i: (0, i)),
        compiler_params=pltpu.CompilerParams(vmem_limit_bytes=40 << 20),
        name="times_transpose",
    )(image, own, other)


def recover(inc, sizes, amp, loads, state, diag, phi, steps):
    load_cols = loads.shape[0]
    tiles = phi.shape[0]
    subs = sizes.shape[0]
    peers, _, frows = amp.shape
    per = frows // BLOCK
    blocks = peers * per
    per_step = tiles // steps
    contract = (((1,), (1,)), ((), ()))

    def kernel(inc_ref, sizes_ref, amp_ref, loads_ref, state_ref, diag_ref, phi_ref, adj_ref, sens_ref, blk_ref, at_ref):
        step = pl.program_id(0)

        @pl.when(step == 0)
        def _():
            for b in range(blocks):
                blk_ref[b] = amp_ref[b // per, :, (b % per) * BLOCK : (b % per + 1) * BLOCK]
            sens_ref[...] = jnp.zeros_like(sens_ref)
            at_ref[0] = 0
            at_ref[1] = sizes_ref[0]

        lane = lax.broadcasted_iota(jnp.int32, (load_cols, subs), 1)
        owner = at_ref[0]
        end = at_ref[1]
        sens = sens_ref[...]
        for j in range(per_step):
            tile = step * per_step + j
            past = (tile >= end) & (owner < subs)
            owner = jnp.where(past, owner + 1, owner)
            end = jnp.where(past & (owner < subs), end + sizes_ref[jnp.minimum(owner, subs - 1)], end)
            live = owner < subs
            here = slice(j * BLOCK, (j + 1) * BLOCK)
            coupling = lax.dot_general(blk_ref[inc_ref[tile]], phi_ref[j], contract, preferred_element_type=F32)
            response = diag_ref[j : j + 1, :] * loads_ref[:, here].astype(F32) + coupling
            response = jnp.where(live, response, jnp.zeros_like(response))
            adj_ref[:, here] = response.astype(BF16)
            total = jnp.sum(response * state_ref[:, here].astype(F32), axis=1, keepdims=True)
            sens = sens + jnp.where(lane == owner, total, jnp.zeros_like(sens))
        sens_ref[...] = jnp.where(step == steps - 1, sens * sens_scale, sens)
        at_ref[0] = owner
        at_ref[1] = end

    return pl.pallas_call(
        kernel,
        out_shape=(
            jax.ShapeDtypeStruct(loads.shape, BF16),
            jax.ShapeDtypeStruct((load_cols, subs), F32),
        ),
        grid_spec=pltpu.PrefetchScalarGridSpec(
            num_scalar_prefetch=2,
            grid=(steps,),
            in_specs=[
                pl.BlockSpec(amp.shape, lambda i, *_: (0, 0, 0)),
                pl.BlockSpec((load_cols, per_step * BLOCK), lambda i, *_: (0, i)),
                pl.BlockSpec((load_cols, per_step * BLOCK), lambda i, *_: (0, i)),
                pl.BlockSpec((per_step, BLOCK), lambda i, *_: (i, 0)),
                pl.BlockSpec((per_step, BLOCK, BLOCK), lambda i, *_: (i, 0, 0)),
            ],
            out_specs=(
                pl.BlockSpec((load_cols, per_step * BLOCK), lambda i, *_: (0, i)),
                pl.BlockSpec((load_cols, subs), lambda i, *_: (0, 0)),
            ),
            scratch_shapes=[
                pltpu.VMEM((blocks, load_cols, BLOCK), BF16),
                pltpu.SMEM((2,), jnp.int32),
            ],
        ),
        compiler_params=pltpu.CompilerParams(vmem_limit_bytes=40 << 20),
        name="recover",
    )(inc, sizes, amp, loads, state, diag, phi)


def exchange(parts, axis):
    return lax.all_to_all(parts, axis, 0, 0, tiled=True)


def total_of(parts):
    return jnp.sum(parts.astype(F32), axis=0).astype(BF16)


def to_all(shard, peers):
    return jnp.broadcast_to(shard[None], (peers, *shard.shape))


def body(loads, state, modal_diag, phi, incidence, sizes, factor):
    load_cols = loads.shape[0]
    wide = lax.axis_size(WIDE)
    deep = lax.axis_size("z")
    frows = factor.shape[0]
    partial, own = condense(incidence, sizes, loads, phi, factor, wide, 8)
    other = lax.ppermute(own, "c", [(0, 1), (1, 0)])
    own_loads = total_of(exchange(partial, WIDE))
    chip_loads = exchange(to_all(own_loads, deep), "z").reshape(deep * load_cols, frows)
    rows = deep * load_cols
    image_part = times_factor(chip_loads, own, other, 4)
    image_part = total_of(exchange(image_part.reshape(wide, rows // wide, -1), WIDE))
    image = exchange(to_all(image_part, wide), WIDE).reshape(rows, -1)
    amp_part = times_transpose(image, own, other, 8)
    amp = total_of(exchange(amp_part.reshape(deep, load_cols, frows), "z"))
    amp_all = exchange(to_all(amp, wide), WIDE)
    diag = modal_diag.reshape(-1, BLOCK)
    return recover(incidence, sizes, amp_all, loads, state, diag, phi, 8)


def solution(mesh):
    fine = Mesh(mesh.devices.reshape(4, 4, 4, 2), ("x", "y", "z", "c"))
    wide, narrow = WIDE, ("z", "c")
    return jax.shard_map(
        body,
        mesh=fine,
        in_specs=(
            P(narrow, wide),
            P(narrow, wide),
            P(wide),
            P(wide, None, None),
            P(wide),
            P(wide),
            P(wide, narrow),
        ),
        out_specs=(P(narrow, wide), P(narrow, wide)),
        check_vma=False,
    )
```

time: 204 us -> 142 us (0.70)
  matrix products: 37.5 us -> 0 us
  Pallas kernels: 0 us -> 34.4 us
  blocking collectives: 120 us -> 97.8 us
  waiting for transfers between devices: 17 us -> 0.01 us
  local copies, waits for them, and re-layouts: 21 us -> 8.13 us
  starting transfers between devices: 3.88 us -> 0.01 us
  other arithmetic: 3 us -> 0.38 us
    dot_general x6 -> x0, matrix products: 37.5 us -> none  [the longest x1 9.73 us: body(): jnp.dot(whole_loads, factor, precision=lax.Precision.HIGHEST)]
    pallas_call x0 -> x4, Pallas kernels: none -> 34.4 us  [the longest x1 12 us: condense(): pl.pallas_call(kernel, out_shape=(jax.ShapeDtypeStruct((peers, load_cols,...]
    all_to_all x5 -> x6, blocking collectives: 120 us -> 97.8 us  [exchange(): return lax.all_to_all(parts, axis, 0, 0, tiled=True)]
    all_to_all x1 -> x0, waiting for transfers between devices: 17 us -> none  [from_everyone(): lax.all_to_all(jnp.broadcast_to(shard[None], (peers, *shard.shape)), axis...]
    unnamed x10 -> x18, local copies, waits for them, and re-layouts: 0.03 us -> 7.9 us
    transpose x3 -> x0, local copies, waits for them, and re-layouts: 7.3 us -> none  [the longest x1 2.94 us: body(): jnp.einsum('tn,ltm->lnm', chooser, tile_terms, precision=lax.Precision.HI...]
    another operation x3 -> x0, local copies, waits for them, and re-layouts: 6.91 us -> none  [the longest x2 4.21 us: body(): amp_all.reshape(load_cols, block_count, block_rows)]
    all_to_all x1 -> x0, starting transfers between devices: 3.88 us -> none  [from_everyone(): lax.all_to_all(jnp.broadcast_to(shard[None], (peers, *shard.shape)), axis...]
  transfers between devices with their start and end apart: 1 -> 1, of which waited for: 1 -> 0; matrix products, arithmetic and copies ran while one was open for 0% -> 0% of each run, Pallas kernels for 0% -> 0%
where the time goes in v1:
time: 142 us; the launch traced here: 141 us
  blocking collectives  97.8 us (69%)
  Pallas kernels  34.4 us (24%)
  local copies, waits for them, and re-layouts  8.13 us (6%)
    all_to_all x6, blocking collectives, exchange(): return lax.all_to_all(parts, axis, 0, 0, tiled=True)  97.8 us
    pallas_call x1, Pallas kernels, condense(): pl.pallas_call(kernel, out_shape=(jax.ShapeDtypeStruct((peers, load_cols,...  12 us
    pallas_call x1, Pallas kernels, recover(): pl.pallas_call(kernel, out_shape=(jax.ShapeDtypeStruct(loads.shape, BF16)...  7.99 us
    unnamed x18, local copies, waits for them, and re-layouts  7.9 us
    pallas_call x1, Pallas kernels, times_transpose(): pl.pallas_call(kernel, out_shape=jax.ShapeDtypeStruct((rows, frows), BF16...  7.35 us
    pallas_call x1, Pallas kernels, times_factor(): pl.pallas_call(kernel, out_shape=jax.ShapeDtypeStruct((rows, 2 * cols), B...  7.08 us
  transfers between devices with their start and end apart: 1, of which 0 were waited for; matrix products, arithmetic and copies ran while one was open for 0% of the time, Pallas kernels for 0%

profile of v1, /device:TPU:0, one launch (start us, length us, event | category | flops | bytes accessed | tf_op | source)
XLA Modules:
  0.0 141.4 jit_solution(4793880882043764990)
XLA Ops:
  0.6 0.0 copy-start.1
  0.6 1.6 %copy-done.1 = bf16[32,32768]{1,0:T(8,128)(2,1)S(1)} copy-done((bf16[32,32768]{1,0:T(8,128)(2,1)S(1)}, bf16[32,32768]{1,0:T(8,128)(2,1)}, u32[]{:S(2)}) %copy-start.1) | copy-done | bytes 2097176
  2.2 0.0 copy-start.5
  2.2 0.7 copy-done.5
  2.9 0.0 copy-start.7
  2.9 0.7 copy-done.7
  3.6 12.0 %condense.1 = (bf16[16,32,1024]{2,1,0:T(8,128)(2,1)S(1)}, bf16[1024,2048]{1,0:T(8,128)(2,1)}) custom-call(s32[256]{0:T(256)S(1)} %copy-done.5, s32[128]{0:T(128)S(1)} %copy-done.7, bf16[32,32768]{1,0:T(8,128)(2,1)S(1)} %copy-done.1, bf16[256,128,128]{2,1,0:T(8,128)(2,1)} %phi_ref.3, f32[1024,2048]{1,0:T(8,128)} %f_ref.1), custom_call_target="tpu_custom_call" | custom-call | tf_op jit(solution)/shard_map/condense/pallas_call | solution.py:44
  15.6 0.0 collective-permute-start
  15.6 24.7 %all_to_all.30 = bf16[16,32,1024]{2,1,0:T(8,128)(2,1)S(1)} all-to-all(bf16[16,32,1024]{2,1,0:T(8,128)(2,1)S(1)} %get-tuple-element.4), channel_id=1, replica_groups=mesh['x'=4,'y'=4,'z'=4,'c'=2] {'x','y'}, dimensions={0} | all-to-all | bytes 2097152 | tf_op jit(solution)/shard_map/all_to_all | solution.py:202
  40.3 0.2 reduce_sum.36
  40.5 11.8 %all_to_all.31 = bf16[4,32,1024]{2,1,0:T(8,128)(2,1)S(1)} all-to-all(bf16[4,32,1024]{2,1,0:T(8,128)(2,1)S(1)} %broadcast_in_dim.6), channel_id=1, replica_groups=mesh['x'=4,'y'=4,'z'=4,'c'=2] {'z'}, dimensions={0} | all-to-all | bytes 524288 | tf_op jit(solution)/shard_map/all_to_all | solution.py:202
  52.3 0.0 collective-permute-done.other_ref
  52.3 7.1 %times_factor.1 = bf16[128,4096]{1,0:T(8,128)(2,1)S(1)} custom-call(bf16[128,1024]{1,0:T(8,128)(2,1)S(1)} %bitcast.7, bf16[1024,2048]{1,0:T(8,128)(2,1)} %get-tuple-element.5.own_ref, bf16[1024,2048]{1,0:T(8,128)(2,1)} %collective-permute-done.other_ref), custom_call_target="tpu_custom_call" | custom-call | tf_op jit(solution)/shard_map/times_factor/pallas_call | solution.py:88
  59.4 18.5 %all_to_all.32 = bf16[16,8,4096]{2,1,0:T(8,128)(2,1)S(1)} all-to-all(bf16[16,8,4096]{2,1,0:T(8,128)(2,1)S(1)} %bitcast.6), channel_id=1, replica_groups=mesh['x'=4,'y'=4,'z'=4,'c'=2] {'x','y'}, dimensions={0} | all-to-all | bytes 2097152 | tf_op jit(solution)/shard_map/all_to_all | solution.py:202
  77.9 0.1 reduce_sum.37
  78.0 0.1 broadcast_in_dim.7
  78.1 17.3 %all_to_all.33 = bf16[16,8,4096]{2,1,0:T(8,128)(2,1)S(1)} all-to-all(bf16[16,8,4096]{2,1,0:T(8,128)(2,1)S(1)} %broadcast_in_dim.7), channel_id=1, replica_groups=mesh['x'=4,'y'=4,'z'=4,'c'=2] {'x','y'}, dimensions={0} | all-to-all | bytes 2097152 | tf_op jit(solution)/shard_map/all_to_all | solution.py:202
  95.4 0.0 copy-start.4
  95.4 0.0 copy-start.6
  95.4 0.0 copy-start.8
  95.4 7.3 %times_transpose.1 = bf16[128,1024]{1,0:T(8,128)(2,1)S(1)} custom-call(bf16[128,4096]{1,0:T(8,128)(2,1)S(1)} %bitcast.5, bf16[1024,2048]{1,0:T(8,128)(2,1)} %get-tuple-element.5.own_ref, bf16[1024,2048]{1,0:T(8,128)(2,1)} %collective-permute-done.other_ref), custom_call_target="tpu_custom_call" | custom-call | tf_op jit(solution)/shard_map/times_transpose/pallas_call | solution.py:114
  102.8 0.0 copy-start.2
  102.8 9.3 %all_to_all.34 = bf16[4,32,1024]{2,1,0:T(8,128)(2,1)S(1)} all-to-all(bf16[4,32,1024]{2,1,0:T(8,128)(2,1)S(1)} %bitcast.8), channel_id=1, replica_groups=mesh['x'=4,'y'=4,'z'=4,'c'=2] {'z'}, dimensions={0} | all-to-all | bytes 524288 | tf_op jit(solution)/shard_map/all_to_all | solution.py:202
  112.1 0.1 broadcast_in_dim.8
  112.3 16.2 %all_to_all.35.amp_ref = bf16[16,32,1024]{2,1,0:T(8,128)(2,1)S(1)} all-to-all(bf16[16,32,1024]{2,1,0:T(8,128)(2,1)S(1)} %broadcast_in_dim.8), channel_id=1, replica_groups=mesh['x'=4,'y'=4,'z'=4,'c'=2] {'x','y'}, dimensions={0} | all-to-all | bytes 2097152 | tf_op jit(solution)/shard_map/all_to_all | solution.py:202
  128.5 0.0 copy-done.4
  128.5 0.0 copy-done.6
  128.5 0.0 copy-done.8
  128.5 0.0 copy-done.2
  128.5 0.0 copy-start
  128.5 3.4 %copy-done = bf16[256,128,128]{2,1,0:T(8,128)(2,1)S(1)} copy-done((bf16[256,128,128]{2,1,0:T(8,128)(2,1)S(1)}, bf16[256,128,128]{2,1,0:T(8,128)(2,1)}, u32[]{:S(2)}) %copy-start) | copy-done | bytes 8388632
  131.9 0.0 copy-start.3
  131.9 1.6 %copy-done.3 = bf16[32,32768]{1,0:T(8,128)(2,1)S(1)} copy-done((bf16[32,32768]{1,0:T(8,128)(2,1)S(1)}, bf16[32,32768]{1,0:T(8,128)(2,1)}, u32[]{:S(2)}) %copy-start.3) | copy-done | bytes 2097176
  133.5 8.0 %recover.1 = (bf16[32,32768]{1,0:T(8,128)(2,1)}, f32[32,128]{1,0:T(8,128)}) custom-call(s32[256]{0:T(256)S(1)} %copy-done.6, s32[128]{0:T(128)S(1)} %copy-done.8, bf16[16,32,1024]{2,1,0:T(8,128)(2,1)S(1)} %all_to_all.35.amp_ref, bf16[32,32768]{1,0:T(8,128)(2,1)S(1)} %copy-done.2, bf16[32,32768]{1,0:T(8,128)(2,1)S(1)} %copy-done.3, f32[256,128]{1,0:T(8,128)S(1)} %bitcast.9, ...), custom_call_target="tpu_custom_call" | custom-call | tf_op jit(solution)/shard_map/recover/pallas_call | solution.py:171
  (2 shorter events, 0.1 us)
Async XLA Ops:
  0.6 1.6 %copy-start.1 = (bf16[32,32768]{1,0:T(8,128)(2,1)S(1)}, bf16[32,32768]{1,0:T(8,128)(2,1)}, u32[]{:S(2)}) copy-start(bf16[32,32768]{1,0:T(8,128)(2,1)} %loads_ref.3) | copy-start | bytes 6291460
  2.2 0.7 copy-start.5
  2.9 0.7 copy-start.7
  15.6 36.7 %collective-permute-start = (bf16[1024,2048]{1,0:T(8,128)(2,1)}, bf16[1024,2048]{1,0:T(8,128)(2,1)}, u32[]{:S(2)}, u32[]{:S(2)}) collective-permute-start(bf16[1024,2048]{1,0:T(8,128)(2,1)} %get-tuple-element.5.own_ref), channel_id=1, source_target_pairs={{0,1},{1,0},{2,3},{3,2},{4,5},{5,4},{6,7},{7,6},{8,9},{9,8},{10,11... | collective-permute-start | bytes 12582920 | tf_op jit(solution)/shard_map/ppermute | solution.py:219
  95.4 33.1 %copy-start.4 = (f32[32768]{0:T(1024)S(1)}, f32[32768]{0:T(1024)}, u32[]{:S(2)}) copy-start(f32[32768]{0:T(1024)} %param.9) | copy-start | bytes 393220
  95.4 33.1 %copy-start.6 = (s32[256]{0:T(256)S(1)}, s32[256]{0:T(256)}, u32[]{:S(2)}) copy-start(s32[256]{0:T(256)} %inc_ref.3) | copy-start | bytes 3076
  95.4 33.1 %copy-start.8 = (s32[128]{0:T(128)S(1)}, s32[128]{0:T(128)}, u32[]{:S(2)}) copy-start(s32[128]{0:T(128)} %sizes_ref.3) | copy-start | bytes 1540
  102.8 25.7 %copy-start.2 = (bf16[32,32768]{1,0:T(8,128)(2,1)S(1)}, bf16[32,32768]{1,0:T(8,128)(2,1)}, u32[]{:S(2)}) copy-start(bf16[32,32768]{1,0:T(8,128)(2,1)} %loads_ref.3) | copy-start | bytes 6291460
  128.5 3.4 %copy-start = (bf16[256,128,128]{2,1,0:T(8,128)(2,1)S(1)}, bf16[256,128,128]{2,1,0:T(8,128)(2,1)}, u32[]{:S(2)}) copy-start(bf16[256,128,128]{2,1,0:T(8,128)(2,1)} %phi_ref.3) | copy-start | bytes 25165828
  131.9 1.6 %copy-start.3 = (bf16[32,32768]{1,0:T(8,128)(2,1)S(1)}, bf16[32,32768]{1,0:T(8,128)(2,1)}, u32[]{:S(2)}) copy-start(bf16[32,32768]{1,0:T(8,128)(2,1)} %state_ref.1) | copy-start | bytes 6291460

commit v2 on v0

v2 whole, which is shorter than its diff:
```python
import jax
import jax.numpy as jnp
from jax import lax
from jax.experimental import pallas as pl
from jax.experimental.pallas import tpu as pltpu
from jax.sharding import Mesh, PartitionSpec as P

sens_scale = 0.0625
BLOCK = 128
WIDE = ("x", "y")
F32, BF16 = jnp.float32, jnp.bfloat16
OUTSIDE = pl.BlockSpec(memory_space=pltpu.HBM)
INSIDE = pl.BlockSpec(memory_space=pltpu.VMEM)
PAIR = 2 * BLOCK


def outside(array):
    return pltpu.with_memory_space_constraint(array, pltpu.HBM)


def room(mib):
    return pltpu.CompilerParams(vmem_limit_bytes=mib << 20)


def condense(inc, sizes, loads, phi, factor, peers, chunks, unroll):
    load_cols = loads.shape[0]
    tiles = phi.shape[0]
    subs = sizes.shape[0]
    frows, fcols = factor.shape
    per = frows // BLOCK
    blocks = peers * per
    some = tiles // chunks
    fsome = frows // chunks

    def kernel(inc_hbm, sizes_hbm, loads_hbm, phi_hbm, f_hbm, out_ref, loads_ref, phi_ref, own_ref, *scratch):
        acc_ref, f_ref, inc_ref, sizes_ref, loads_sem, phi_sem, f_sem, scalar_sem = scratch

        def loads_copy(c):
            cols = pl.ds(c * some * BLOCK, some * BLOCK)
            return pltpu.make_async_copy(loads_hbm.at[:, cols], loads_ref.at[:, cols], loads_sem.at[c])

        def phi_copy(c):
            rows = pl.ds(c * some, some)
            return pltpu.make_async_copy(phi_hbm.at[rows], phi_ref.at[rows], phi_sem.at[c])

        def f_copy(c):
            rows = pl.ds(c * fsome, fsome)
            return pltpu.make_async_copy(f_hbm.at[rows], f_ref.at[rows], f_sem.at[c])

        inc_copy = pltpu.make_async_copy(inc_hbm, inc_ref, scalar_sem.at[0])
        sizes_copy = pltpu.make_async_copy(sizes_hbm, sizes_ref, scalar_sem.at[1])
        sizes_copy.start()
        inc_copy.start()
        for c in range(chunks):
            loads_copy(c).start()
            phi_copy(c).start()
            f_copy(c).start()
        acc_ref[...] = jnp.zeros_like(acc_ref)
        sizes_copy.wait()
        live = lax.fori_loop(0, subs, lambda s, n: n + sizes_ref[s], jnp.int32(0), unroll=16)
        inc_copy.wait()

        def part(p, carry):
            for j in range(0, unroll, 2):
                tile = p * unroll + j
                if j % some == 0:
                    c = p * (unroll // some) + j // some
                    loads_copy(c).wait()
                    phi_copy(c).wait()
                cols = pl.multiple_of(tile * BLOCK, PAIR)
                rows = jnp.concatenate([loads_ref[:, pl.ds(cols, BLOCK)], loads_ref[:, pl.ds(cols + BLOCK, BLOCK)]], axis=0)
                both = jnp.concatenate([phi_ref[tile], phi_ref[tile + 1]], axis=1)
                terms = jnp.dot(rows, both, preferred_element_type=F32)
                first, second = terms[:load_cols, :BLOCK], terms[load_cols:, BLOCK:]
                acc_ref[inc_ref[tile]] += jnp.where(tile < live, first, jnp.zeros_like(first))
                acc_ref[inc_ref[tile + 1]] += jnp.where(tile + 1 < live, second, jnp.zeros_like(second))
            for i in range(unroll // some):
                c = p * (unroll // some) + i
                f_copy(c).wait()
                rows = pl.ds(c * fsome, fsome)
                own_ref[rows] = f_ref[rows].astype(BF16)
            return carry

        lax.fori_loop(0, tiles // unroll, part, 0)
        for b in range(blocks):
            out_ref[b // per, :, (b % per) * BLOCK : (b % per + 1) * BLOCK] = acc_ref[b].astype(BF16)

    return pl.pallas_call(
        kernel,
        out_shape=(
            jax.ShapeDtypeStruct((peers, load_cols, frows), BF16),
            pltpu.VMEM(loads.shape, BF16),
            pltpu.VMEM(phi.shape, BF16),
            pltpu.VMEM(factor.shape, BF16),
        ),
        in_specs=[OUTSIDE] * 5,
        out_specs=(INSIDE,) * 4,
        scratch_shapes=[
            pltpu.VMEM((blocks, load_cols, BLOCK), F32),
            pltpu.VMEM(factor.shape, F32),
            pltpu.SMEM(inc.shape, jnp.int32),
            pltpu.SMEM(sizes.shape, jnp.int32),
            pltpu.SemaphoreType.DMA((chunks,)),
            pltpu.SemaphoreType.DMA((chunks,)),
            pltpu.SemaphoreType.DMA((chunks,)),
            pltpu.SemaphoreType.DMA((2,)),
        ],
        compiler_params=room(12),
        name="condense",
    )(*[outside(a) for a in (inc, sizes, loads, phi, factor)])


def total_of(parts, copies):
    shape = parts[0].shape[1:] if len(parts) == 1 else parts[0].shape

    def kernel(*refs):
        *part_refs, out_ref = refs
        if len(parts) == 1:
            terms = [part_refs[0][i] for i in range(parts[0].shape[0])]
        else:
            terms = [r[...] for r in part_refs]
        total = terms[0].astype(F32)
        for term in terms[1:]:
            total += term.astype(F32)
        total = total.astype(BF16)
        if copies:
            for i in range(copies):
                out_ref[i] = total
        else:
            out_ref[...] = total

    return pl.pallas_call(
        kernel,
        out_shape=jax.ShapeDtypeStruct((copies, *shape) if copies else shape, BF16),
        in_specs=[INSIDE] * len(parts),
        out_specs=INSIDE,
        compiler_params=room(4),
        name="total_of",
    )(*parts)


def times_factor(parts, own, other, width):
    rows = len(parts) * parts[0].shape[0]
    cols = own.shape[1]

    def kernel(*refs):
        *part_refs, own_ref, other_ref, out_ref = refs
        left = jnp.concatenate([r[...] for r in part_refs], axis=0)
        for at, half_ref in ((0, own_ref), (cols, other_ref)):
            for c in range(0, cols, width):
                product = jnp.dot(left, half_ref[:, c : c + width], preferred_element_type=F32)
                out_ref[:, at + c : at + c + width] = product.astype(BF16)

    return pl.pallas_call(
        kernel,
        out_shape=jax.ShapeDtypeStruct((rows, 2 * cols), BF16),
        in_specs=[INSIDE] * (len(parts) + 2),
        out_specs=INSIDE,
        compiler_params=room(8),
        name="times_factor",
    )(*parts, own, other)


def times_transpose(image, own, other, groups, height):
    rows = image.shape[0]
    frows, cols = own.shape
    group = rows // groups
    contract = (((1,), (1,)), ((), ()))

    def kernel(image_ref, own_ref, other_ref, *outs):
        for c in range(frows // height):
            some = slice(c * height, (c + 1) * height)
            total = lax.dot_general(image_ref[:, :cols], own_ref[some], contract, preferred_element_type=F32)
            total += lax.dot_general(image_ref[:, cols:], other_ref[some], contract, preferred_element_type=F32)
            for g in range(groups):
                outs[g][:, some] = total[g * group : (g + 1) * group].astype(BF16)

    return pl.pallas_call(
        kernel,
        out_shape=[jax.ShapeDtypeStruct((group, frows), BF16)] * groups,
        in_specs=[INSIDE] * 3,
        out_specs=[INSIDE] * groups,
        compiler_params=room(8),
        name="times_transpose",
    )(image, own, other)


def recover(inc, sizes, amp, loads, state, diag, phi, unroll):
    load_cols = loads.shape[0]
    tiles = phi.shape[0]
    subs = sizes.shape[0]
    peers, _, frows = amp.shape
    per = frows // BLOCK
    blocks = peers * per
    parts = tiles // unroll
    contract = (((1,), (1,)), ((), ()))

    def kernel(inc_hbm, sizes_hbm, amp_ref, loads_ref, state_ref, diag_ref, phi_ref, adj_hbm, sens_ref, *scratch):
        adj_ref, blk_ref, inc_ref, sizes_ref, sem, scalar_sem = scratch
        inc_copy = pltpu.make_async_copy(inc_hbm, inc_ref, scalar_sem.at[0])
        sizes_copy = pltpu.make_async_copy(sizes_hbm, sizes_ref, scalar_sem.at[1])
        inc_copy.start()
        sizes_copy.start()
        for b in range(blocks):
            blk_ref[b] = amp_ref[b // per, :, (b % per) * BLOCK : (b % per + 1) * BLOCK]
        lane = lax.broadcasted_iota(jnp.int32, (load_cols, subs), 1)
        inc_copy.wait()
        sizes_copy.wait()

        def adj_copy(p):
            cols = pl.ds(pl.multiple_of(p * unroll * BLOCK, BLOCK), unroll * BLOCK)
            return pltpu.make_async_copy(adj_ref.at[:, cols], adj_hbm.at[:, cols], sem.at[p])

        def part(p, carry):
            owner, end, sens = carry
            for j in range(0, unroll, 2):
                tile = p * unroll + j
                rows = jnp.concatenate([blk_ref[inc_ref[tile]], blk_ref[inc_ref[tile + 1]]], axis=0)
                both = phi_ref[pl.ds(tile, 2)].reshape(PAIR, BLOCK)
                product = lax.dot_general(rows, both, contract, preferred_element_type=F32)
                couplings = (product[:load_cols, :BLOCK], product[load_cols:, BLOCK:])
                for q, coupling in enumerate(couplings):
                    past = (tile + q >= end) & (owner < subs)
                    owner = jnp.where(past, owner + 1, owner)
                    end = jnp.where(past & (owner < subs), end + sizes_ref[jnp.minimum(owner, subs - 1)], end)
                    cols = pl.ds(pl.multiple_of((tile + q) * BLOCK, BLOCK), BLOCK)
                    response = diag_ref[pl.ds(tile + q, 1), :] * loads_ref[:, cols].astype(F32) + coupling
                    response = jnp.where(owner < subs, response, jnp.zeros_like(response))
                    adj_ref[:, cols] = response.astype(BF16)
                    total = jnp.sum(response * state_ref[:, cols].astype(F32), axis=1, keepdims=True)
                    sens = sens + jnp.where(lane == owner, total, jnp.zeros_like(sens))
            adj_copy(p).start()
            return owner, end, sens

        start = (jnp.int32(0), sizes_ref[0], jnp.zeros((load_cols, subs), F32))
        _, _, sens = lax.fori_loop(0, parts, part, start)
        sens_ref[...] = sens * sens_scale
        for p in range(parts):
            adj_copy(p).wait()

    return pl.pallas_call(
        kernel,
        out_shape=(
            jax.ShapeDtypeStruct(loads.shape, BF16),
            jax.ShapeDtypeStruct((load_cols, subs), F32),
        ),
        in_specs=[OUTSIDE] * 2 + [INSIDE] * 5,
        out_specs=(OUTSIDE, INSIDE),
        scratch_shapes=[
            pltpu.VMEM(loads.shape, BF16),
            pltpu.VMEM((blocks, load_cols, BLOCK), BF16),
            pltpu.SMEM(inc.shape, jnp.int32),
            pltpu.SMEM(sizes.shape, jnp.int32),
            pltpu.SemaphoreType.DMA((parts,)),
            pltpu.SemaphoreType.DMA((2,)),
        ],
        compiler_params=room(6),
        name="recover",
    )(inc, sizes, amp, loads, state, diag, phi)


def exchange(parts, axis):
    return lax.all_to_all(parts, axis, 0, 0, tiled=True)


def moved(value, axis, by):
    peers = lax.axis_size(axis)
    return lax.ppermute(value, axis, [(i, (i + by) % peers) for i in range(peers)])


def body(loads, state, modal_diag, phi, incidence, sizes, factor):
    wide = lax.axis_size(WIDE)
    frows = factor.shape[0]
    shifts = (1, 3, 2)
    partial, loads_in, phi_in, own = condense(incidence, sizes, loads, phi, factor, wide, 8, 64)
    other = moved(own, "c", 1)
    own_loads = total_of([exchange(partial, WIDE)], 0)
    chip_loads = [own_loads] + [moved(own_loads, "z", s) for s in shifts]
    image_part = times_factor(chip_loads, own, other, 512)
    rows = image_part.shape[0]
    image_parts = exchange(image_part.reshape(wide, rows // wide, -1), WIDE)
    image = exchange(total_of([image_parts], wide), WIDE).reshape(rows, -1)
    diag = modal_diag.reshape(-1, BLOCK)
    amp_parts = times_transpose(image, own, other, 4, 128)
    amp_parts = [amp_parts[0]] + [moved(a, "z", -s) for a, s in zip(amp_parts[1:], shifts)]
    amp_all = exchange(total_of(amp_parts, wide), WIDE)
    return recover(incidence, sizes, amp_all, loads_in, state, diag, phi_in, 64)


def solution(mesh):
    fine = Mesh(mesh.devices.reshape(4, 4, 4, 2), ("x", "y", "z", "c"))
    wide, narrow = WIDE, ("z", "c")
    return jax.shard_map(
        body,
        mesh=fine,
        in_specs=(
            P(narrow, wide),
            P(narrow, wide),
            P(wide),
            P(wide, None, None),
            P(wide),
            P(wide),
            P(wide, narrow),
        ),
        out_specs=(P(narrow, wide), P(narrow, wide)),
        check_vma=False,
    )
```

time: 204 us -> 112 us (0.55)
  blocking collectives: 120 us -> 76 us
  matrix products: 37.5 us -> 0 us
  local copies, waits for them, and re-layouts: 21 us -> 0.01 us
  Pallas kernels: 0 us -> 16.8 us
  waiting for transfers between devices: 17 us -> 8 us
  starting transfers between devices: 3.88 us -> 10.1 us
  other arithmetic: 3 us -> 0 us
    all_to_all x5 -> x4, blocking collectives: 120 us -> 76 us  [exchange(): return lax.all_to_all(parts, axis, 0, 0, tiled=True)]
    dot_general x6 -> x0, matrix products: 37.5 us -> none  [the longest x1 9.73 us: body(): jnp.dot(whole_loads, factor, precision=lax.Precision.HIGHEST)]
    all_to_all x1 -> x0, waiting for transfers between devices: 17 us -> none  [from_everyone(): lax.all_to_all(jnp.broadcast_to(shard[None], (peers, *shard.shape)), axis...]
    pallas_call x0 -> x7, Pallas kernels: none -> 16.8 us  [the longest x1 6.9 us: condense(): pl.pallas_call(kernel, out_shape=(jax.ShapeDtypeStruct((peers, load_cols,...]
    ppermute x0 -> x7, starting transfers between devices: none -> 10.1 us  [moved(): lax.ppermute(value, axis, [(i, (i + by) % peers) for i in range(peers)])]
    ppermute x0 -> x7, waiting for transfers between devices: none -> 8 us  [moved(): lax.ppermute(value, axis, [(i, (i + by) % peers) for i in range(peers)])]
    transpose x3 -> x0, local copies, waits for them, and re-layouts: 7.3 us -> none  [the longest x1 2.94 us: body(): jnp.einsum('tn,ltm->lnm', chooser, tile_terms, precision=lax.Precision.HI...]
    another operation x3 -> x0, local copies, waits for them, and re-layouts: 6.91 us -> none  [the longest x2 4.21 us: body(): amp_all.reshape(load_cols, block_count, block_rows)]
  transfers between devices with their start and end apart: 1 -> 7, of which waited for: 1 -> 6; matrix products, arithmetic and copies ran while one was open for 0% -> 0% of each run, Pallas kernels for 0% -> 0%
where the time goes in v2:
time: 112 us
  blocking collectives  76 us (68%)
  Pallas kernels  16.8 us (15%)
  starting transfers between devices  10.1 us (9%)
  waiting for transfers between devices  8 us (7%)
    all_to_all x4, blocking collectives, exchange(): return lax.all_to_all(parts, axis, 0, 0, tiled=True)  76 us
    ppermute x7, starting transfers between devices, moved(): lax.ppermute(value, axis, [(i, (i + by) % peers) for i in range(peers)])  10.1 us
    ppermute x7, waiting for transfers between devices, moved(): lax.ppermute(value, axis, [(i, (i + by) % peers) for i in range(peers)])  8 us
    pallas_call x1, Pallas kernels, condense(): pl.pallas_call(kernel, out_shape=(jax.ShapeDtypeStruct((peers, load_cols,...  6.9 us
    pallas_call x1, Pallas kernels, recover(): pl.pallas_call(kernel, out_shape=(jax.ShapeDtypeStruct(loads.shape, BF16)...  5.94 us
    pallas_call x1, Pallas kernels, times_transpose(): pl.pallas_call(kernel, out_shape=[jax.ShapeDtypeStruct((group, frows), BF...  2.33 us
  transfers between devices with their start and end apart: 7, of which 6 were waited for; matrix products, arithmetic and copies ran while one was open for 0% of the time, Pallas kernels for 0%

profile of v2, /device:TPU:0, one launch (start us, length us, event | category | flops | bytes accessed | tf_op | source)
XLA Modules:
  0.0 111.6 jit_solution(9350688284235599744)
XLA Ops:
  0.6 6.9 %condense.1 = (bf16[16,32,1024]{2,1,0:T(8,128)(2,1)S(1)}, bf16[32,32768]{1,0:T(8,128)(2,1)S(1)}, bf16[256,128,128]{2,1,0:T(8,128)(2,1)S(1)}, bf16[1024,2048]{1,0:T(8,128)(2,1)S(1)}) custom-call(s32[256]{0:T(256)} %inc_hbm.3, s32[128]{0:T(128)} %sizes_hbm.3, bf16[32,32768]{1,0:T(8,128)(2,1)} %loads_hbm.1, bf16[256,128,128]{2,1,0:T(8,128)(2,1)} %phi_hbm.1, ...), custom_call_target="tpu_custom_call" | custom-call | tf_op jit(solution)/shard_map/condense/pallas_call | solution.py:88
  7.5 0.1 collective-permute-start.3
  7.6 24.7 %all_to_all.20.refs_0_ = bf16[16,32,1024]{2,1,0:T(8,128)(2,1)S(1)} all-to-all(bf16[16,32,1024]{2,1,0:T(8,128)(2,1)S(1)} %get-tuple-element.10), channel_id=1, replica_groups=mesh['x'=4,'y'=4,'z'=4,'c'=2] {'x','y'}, dimensions={0} | all-to-all | bytes 2097152 | tf_op jit(solution)/shard_map/all_to_all | solution.py:263
  32.3 0.1 total_of.3.refs_0_
  32.5 4.0 %collective-permute-start.2 = (bf16[32,1024]{1,0:T(8,128)(2,1)S(1)}, bf16[32,1024]{1,0:T(8,128)(2,1)S(1)}, u32[]{:S(2)}, u32[]{:S(2)}) collective-permute-start(bf16[32,1024]{1,0:T(8,128)(2,1)S(1)} %total_of.3.refs_0_), channel_id=1, source_target_pairs={{0,4},{2,6},{4,0},{6,2},{1,5},{3,7},{5,1},{7,3},{8,12},{10,14},{12... | collective-permute-start | bytes 196616 | tf_op jit(solution)/shard_map/ppermute | solution.py:268
  36.4 0.7 collective-permute-start.1
  37.1 1.3 %collective-permute-start = (bf16[32,1024]{1,0:T(8,128)(2,1)S(1)}, bf16[32,1024]{1,0:T(8,128)(2,1)S(1)}, u32[]{:S(2)}, u32[]{:S(2)}) collective-permute-start(bf16[32,1024]{1,0:T(8,128)(2,1)S(1)} %total_of.3.refs_0_), channel_id=1, source_target_pairs={{0,2},{2,4},{4,6},{6,0},{1,3},{3,5},{5,7},{7,1},{8,10},{10,12},{12... | collective-permute-start | bytes 196616 | tf_op jit(solution)/shard_map/ppermute | solution.py:268
  38.4 0.9 collective-permute-done.2.refs_3_
  39.3 1.4 %collective-permute-done.1.refs_2_ = bf16[32,1024]{1,0:T(8,128)(2,1)S(1)} collective-permute-done((bf16[32,1024]{1,0:T(8,128)(2,1)S(1)}, bf16[32,1024]{1,0:T(8,128)(2,1)S(1)}, u32[]{:S(2)}, u32[]{:S(2)}) %collective-permute-start.1) | collective-permute-done | bytes 65568 | tf_op jit(solution)/shard_map/ppermute | solution.py:268
  40.7 1.9 %collective-permute-done.refs_1_ = bf16[32,1024]{1,0:T(8,128)(2,1)S(1)} collective-permute-done((bf16[32,1024]{1,0:T(8,128)(2,1)S(1)}, bf16[32,1024]{1,0:T(8,128)(2,1)S(1)}, u32[]{:S(2)}, u32[]{:S(2)}) %collective-permute-start) | collective-permute-done | bytes 65568 | tf_op jit(solution)/shard_map/ppermute | solution.py:268
  42.6 0.0 collective-permute-done.3.refs_5_.other_ref
  42.6 1.3 %times_factor.1 = bf16[128,4096]{1,0:T(8,128)(2,1)S(1)} custom-call(bf16[32,1024]{1,0:T(8,128)(2,1)S(1)} %total_of.3.refs_0_, bf16[32,1024]{1,0:T(8,128)(2,1)S(1)} %collective-permute-done.refs_1_, bf16[32,1024]{1,0:T(8,128)(2,1)S(1)} %collective-permute-done.1.refs_2_, bf16[32,1024]{1,0:T(8,128)(2,1)S(1)} %collective-permute-done.2.refs_3_, ...), custom_call_target="tpu_custom_call" | custom-call | tf_op jit(solution)/shard_map/times_factor/pallas_call | solution.py:154
  43.9 18.2 %all_to_all.21.refs_0_ = bf16[16,8,4096]{2,1,0:T(8,128)(2,1)S(1)} all-to-all(bf16[16,8,4096]{2,1,0:T(8,128)(2,1)S(1)} %bitcast.4), channel_id=1, replica_groups=mesh['x'=4,'y'=4,'z'=4,'c'=2] {'x','y'}, dimensions={0} | all-to-all | bytes 2097152 | tf_op jit(solution)/shard_map/all_to_all | solution.py:263
  62.1 0.2 total_of.4
  62.2 17.0 %all_to_all.22 = bf16[16,8,4096]{2,1,0:T(8,128)(2,1)S(1)} all-to-all(bf16[16,8,4096]{2,1,0:T(8,128)(2,1)S(1)} %total_of.4), channel_id=1, replica_groups=mesh['x'=4,'y'=4,'z'=4,'c'=2] {'x','y'}, dimensions={0} | all-to-all | bytes 2097152 | tf_op jit(solution)/shard_map/all_to_all | solution.py:263
  79.2 0.0 copy-start
  79.2 0.0 copy-start.1
  79.2 0.0 copy-start.2
  79.2 0.0 copy-start.3
  79.2 2.3 %times_transpose.1 = (bf16[32,1024]{1,0:T(8,128)(2,1)S(1)}, bf16[32,1024]{1,0:T(8,128)(2,1)S(1)}, bf16[32,1024]{1,0:T(8,128)(2,1)S(1)}, bf16[32,1024]{1,0:T(8,128)(2,1)S(1)}) custom-call(bf16[128,4096]{1,0:T(8,128)(2,1)S(1)} %bitcast.3, bf16[1024,2048]{1,0:T(8,128)(2,1)S(1)} %get-tuple-element.11.refs_4_.own_ref, ...), custom_call_target="tpu_custom_call" | custom-call | tf_op jit(solution)/shard_map/times_transpose/pallas_call | solution.py:178
  81.5 1.6 %collective-permute-start.4 = (bf16[32,1024]{1,0:T(8,128)(2,1)S(1)}, bf16[32,1024]{1,0:T(8,128)(2,1)S(1)}, u32[]{:S(2)}, u32[]{:S(2)}) collective-permute-start(bf16[32,1024]{1,0:T(8,128)(2,1)S(1)} %get-tuple-element.13), channel_id=1, source_target_pairs={{0,6},{2,0},{4,2},{6,4},{1,7},{3,1},{5,3},{7,5},{8,14},{10,8},{12,... | collective-permute-start | bytes 196616 | tf_op jit(solution)/shard_map/ppermute | solution.py:268
  83.2 0.5 collective-permute-start.5
  83.6 1.9 %collective-permute-start.6 = (bf16[32,1024]{1,0:T(8,128)(2,1)S(1)}, bf16[32,1024]{1,0:T(8,128)(2,1)S(1)}, u32[]{:S(2)}, u32[]{:S(2)}) collective-permute-start(bf16[32,1024]{1,0:T(8,128)(2,1)S(1)} %get-tuple-element.15), channel_id=1, source_target_pairs={{0,4},{2,6},{4,0},{6,2},{1,5},{3,7},{5,1},{7,3},{8,12},{10,14},{12... | collective-permute-start | bytes 196616 | tf_op jit(solution)/shard_map/ppermute | solution.py:268
  85.6 0.3 collective-permute-done.4.refs_1_
  85.9 2.8 %collective-permute-done.5.refs_2_ = bf16[32,1024]{1,0:T(8,128)(2,1)S(1)} collective-permute-done((bf16[32,1024]{1,0:T(8,128)(2,1)S(1)}, bf16[32,1024]{1,0:T(8,128)(2,1)S(1)}, u32[]{:S(2)}, u32[]{:S(2)}) %collective-permute-start.5) | collective-permute-done | bytes 65568 | tf_op jit(solution)/shard_map/ppermute | solution.py:268
  88.7 0.8 collective-permute-done.6.refs_3_
  89.4 0.1 total_of.5
  89.5 16.2 %all_to_all.23.amp_ref = bf16[16,32,1024]{2,1,0:T(8,128)(2,1)S(1)} all-to-all(bf16[16,32,1024]{2,1,0:T(8,128)(2,1)S(1)} %total_of.5), channel_id=1, replica_groups=mesh['x'=4,'y'=4,'z'=4,'c'=2] {'x','y'}, dimensions={0} | all-to-all | bytes 2097152 | tf_op jit(solution)/shard_map/all_to_all | solution.py:263
  105.7 0.0 copy-done
  105.7 0.0 copy-done.1
  105.7 0.0 copy-done.2
  105.7 0.0 copy-done.3
  105.7 5.9 %recover.1 = (bf16[32,32768]{1,0:T(8,128)(2,1)}, f32[32,128]{1,0:T(8,128)}) custom-call(s32[256]{0:T(256)S(1)} %copy-done.2, s32[128]{0:T(128)S(1)} %copy-done.3, bf16[16,32,1024]{2,1,0:T(8,128)(2,1)S(1)} %all_to_all.23.amp_ref, bf16[32,32768]{1,0:T(8,128)(2,1)S(1)} %get-tuple-element.16.loads_ref, bf16[32,32768]{1,0:T(8,128)(2,1)S(1)} %copy-done, ...), custom_call_target="tpu_custom_call" | custom-call | tf_op jit(solution)/shard_map/recover/pallas_call | solution.py:241
Async XLA Ops:
  7.5 35.1 %collective-permute-start.3 = (bf16[1024,2048]{1,0:T(8,128)(2,1)S(1)}, bf16[1024,2048]{1,0:T(8,128)(2,1)S(1)}, u32[]{:S(2)}, u32[]{:S(2)}) collective-permute-start(bf16[1024,2048]{1,0:T(8,128)(2,1)S(1)} %get-tuple-element.11.refs_4_.own_ref), channel_id=1, source_target_pairs={{0,1},{1,0},{2,3},{3,2},{4,5},{5,4},{6,7},{7,6},{8,9},{9,8},{10,11... | collective-permute-start | bytes 12582920 | tf_op jit(solution)/shard_map/ppermute | solution.py:268
  32.5 6.9 %collective-permute-start.2 = (bf16[32,1024]{1,0:T(8,128)(2,1)S(1)}, bf16[32,1024]{1,0:T(8,128)(2,1)S(1)}, u32[]{:S(2)}, u32[]{:S(2)}) collective-permute-start(bf16[32,1024]{1,0:T(8,128)(2,1)S(1)} %total_of.3.refs_0_), channel_id=1, source_target_pairs={{0,4},{2,6},{4,0},{6,2},{1,5},{3,7},{5,1},{7,3},{8,12},{10,14},{12... | collective-permute-start | bytes 196616 | tf_op jit(solution)/shard_map/ppermute | solution.py:268
  36.4 4.3 %collective-permute-start.1 = (bf16[32,1024]{1,0:T(8,128)(2,1)S(1)}, bf16[32,1024]{1,0:T(8,128)(2,1)S(1)}, u32[]{:S(2)}, u32[]{:S(2)}) collective-permute-start(bf16[32,1024]{1,0:T(8,128)(2,1)S(1)} %total_of.3.refs_0_), channel_id=1, source_target_pairs={{0,6},{2,0},{4,2},{6,4},{1,7},{3,1},{5,3},{7,5},{8,14},{10,8},{12,... | collective-permute-start | bytes 196616 | tf_op jit(solution)/shard_map/ppermute | solution.py:268
  37.1 5.5 %collective-permute-start = (bf16[32,1024]{1,0:T(8,128)(2,1)S(1)}, bf16[32,1024]{1,0:T(8,128)(2,1)S(1)}, u32[]{:S(2)}, u32[]{:S(2)}) collective-permute-start(bf16[32,1024]{1,0:T(8,128)(2,1)S(1)} %total_of.3.refs_0_), channel_id=1, source_target_pairs={{0,2},{2,4},{4,6},{6,0},{1,3},{3,5},{5,7},{7,1},{8,10},{10,12},{12... | collective-permute-start | bytes 196616 | tf_op jit(solution)/shard_map/ppermute | solution.py:268
  79.2 26.5 %copy-start = (bf16[32,32768]{1,0:T(8,128)(2,1)S(1)}, bf16[32,32768]{1,0:T(8,128)(2,1)}, u32[]{:S(2)}) copy-start(bf16[32,32768]{1,0:T(8,128)(2,1)} %state_ref.1) | copy-start | bytes 6291460
  79.2 26.5 %copy-start.1 = (f32[32768]{0:T(1024)S(1)}, f32[32768]{0:T(1024)}, u32[]{:S(2)}) copy-start(f32[32768]{0:T(1024)} %param.9) | copy-start | bytes 393220
  79.2 26.5 %copy-start.2 = (s32[256]{0:T(256)S(1)}, s32[256]{0:T(256)}, u32[]{:S(2)}) copy-start(s32[256]{0:T(256)} %inc_hbm.3) | copy-start | bytes 3076
  79.2 26.5 %copy-start.3 = (s32[128]{0:T(128)S(1)}, s32[128]{0:T(128)}, u32[]{:S(2)}) copy-start(s32[128]{0:T(128)} %sizes_hbm.3) | copy-start | bytes 1540
  81.5 4.3 %collective-permute-start.4 = (bf16[32,1024]{1,0:T(8,128)(2,1)S(1)}, bf16[32,1024]{1,0:T(8,128)(2,1)S(1)}, u32[]{:S(2)}, u32[]{:S(2)}) collective-permute-start(bf16[32,1024]{1,0:T(8,128)(2,1)S(1)} %get-tuple-element.13), channel_id=1, source_target_pairs={{0,6},{2,0},{4,2},{6,4},{1,7},{3,1},{5,3},{7,5},{8,14},{10,8},{12,... | collective-permute-start | bytes 196616 | tf_op jit(solution)/shard_map/ppermute | solution.py:268
  83.2 5.5 %collective-permute-start.5 = (bf16[32,1024]{1,0:T(8,128)(2,1)S(1)}, bf16[32,1024]{1,0:T(8,128)(2,1)S(1)}, u32[]{:S(2)}, u32[]{:S(2)}) collective-permute-start(bf16[32,1024]{1,0:T(8,128)(2,1)S(1)} %get-tuple-element.14), channel_id=1, source_target_pairs={{0,2},{2,4},{4,6},{6,0},{1,3},{3,5},{5,7},{7,1},{8,10},{10,12},{12... | collective-permute-start | bytes 196616 | tf_op jit(solution)/shard_map/ppermute | solution.py:268
  83.6 5.8 %collective-permute-start.6 = (bf16[32,1024]{1,0:T(8,128)(2,1)S(1)}, bf16[32,1024]{1,0:T(8,128)(2,1)S(1)}, u32[]{:S(2)}, u32[]{:S(2)}) collective-permute-start(bf16[32,1024]{1,0:T(8,128)(2,1)S(1)} %get-tuple-element.15), channel_id=1, source_target_pairs={{0,4},{2,6},{4,0},{6,2},{1,5},{3,7},{5,1},{7,3},{8,12},{10,14},{12... | collective-permute-start | bytes 196616 | tf_op jit(solution)/shard_map/ppermute | solution.py:268

commit v3 on v2

--- a/solution.py
+++ b/solution.py
@@ -22,18 +22,16 @@
     return pltpu.CompilerParams(vmem_limit_bytes=mib << 20)
 
 
-def condense(inc, sizes, loads, phi, factor, peers, chunks, unroll):
+def condense(inc, sizes, loads, phi, peers, frows, chunks, unroll):
     load_cols = loads.shape[0]
     tiles = phi.shape[0]
     subs = sizes.shape[0]
-    frows, fcols = factor.shape
     per = frows // BLOCK
     blocks = peers * per
     some = tiles // chunks
-    fsome = frows // chunks
-
-    def kernel(inc_hbm, sizes_hbm, loads_hbm, phi_hbm, f_hbm, out_ref, loads_ref, phi_ref, own_ref, *scratch):
-        acc_ref, f_ref, inc_ref, sizes_ref, loads_sem, phi_sem, f_sem, scalar_sem = scratch
+
+    def kernel(inc_hbm, sizes_hbm, loads_hbm, phi_hbm, out_ref, loads_ref, phi_ref, *scratch):
+        acc_ref, inc_ref, sizes_ref, loads_sem, phi_sem, scalar_sem = scratch
 
         def loads_copy(c):
             cols = pl.ds(c * some * BLOCK, some * BLOCK)
@@ -42,10 +40,6 @@
         def phi_copy(c):
             rows = pl.ds(c * some, some)
             return pltpu.make_async_copy(phi_hbm.at[rows], phi_ref.at[rows], phi_sem.at[c])
-
-        def f_copy(c):
-            rows = pl.ds(c * fsome, fsome)
-            return pltpu.make_async_copy(f_hbm.at[rows], f_ref.at[rows], f_sem.at[c])
 
         inc_copy = pltpu.make_async_copy(inc_hbm, inc_ref, scalar_sem.at[0])
         sizes_copy = pltpu.make_async_copy(sizes_hbm, sizes_ref, scalar_sem.at[1])
@@ -54,7 +48,6 @@
         for c in range(chunks):
             loads_copy(c).start()
             phi_copy(c).start()
-            f_copy(c).start()
         acc_ref[...] = jnp.zeros_like(acc_ref)
         sizes_copy.wait()
         live = lax.fori_loop(0, subs, lambda s, n: n + sizes_ref[s], jnp.int32(0), unroll=16)
@@ -74,11 +67,6 @@
                 first, second = terms[:load_cols, :BLOCK], terms[load_cols:, BLOCK:]
                 acc_ref[inc_ref[tile]] += jnp.where(tile < live, first, jnp.zeros_like(first))
                 acc_ref[inc_ref[tile + 1]] += jnp.where(tile + 1 < live, second, jnp.zeros_like(second))
-            for i in range(unroll // some):
-                c = p * (unroll // some) + i
-                f_copy(c).wait()
-                rows = pl.ds(c * fsome, fsome)
-                own_ref[rows] = f_ref[rows].astype(BF16)
             return carry
 
         lax.fori_loop(0, tiles // unroll, part, 0)
@@ -91,23 +79,36 @@
             jax.ShapeDtypeStruct((peers, load_cols, frows), BF16),
             pltpu.VMEM(loads.shape, BF16),
             pltpu.VMEM(phi.shape, BF16),
-            pltpu.VMEM(factor.shape, BF16),
         ),
-        in_specs=[OUTSIDE] * 5,
-        out_specs=(INSIDE,) * 4,
+        in_specs=[OUTSIDE] * 4,
+        out_specs=(INSIDE,) * 3,
         scratch_shapes=[
             pltpu.VMEM((blocks, load_cols, BLOCK), F32),
-            pltpu.VMEM(factor.shape, F32),
             pltpu.SMEM(inc.shape, jnp.int32),
             pltpu.SMEM(sizes.shape, jnp.int32),
             pltpu.SemaphoreType.DMA((chunks,)),
             pltpu.SemaphoreType.DMA((chunks,)),
-            pltpu.SemaphoreType.DMA((chunks,)),
             pltpu.SemaphoreType.DMA((2,)),
         ],
-        compiler_params=room(12),
+        compiler_params=room(4),
         name="condense",
-    )(*[outside(a) for a in (inc, sizes, loads, phi, factor)])
+    )(*[outside(a) for a in (inc, sizes, loads, phi)])
+
+
+def rounded(own, other, after):
+    def kernel(own_ref, other_ref, after_ref, own_out, other_out):
+        own_out[...] = own_ref[...].astype(BF16)
+        other_out[...] = other_ref[...].astype(BF16)
+
+    return pl.pallas_call(
+        kernel,
+        out_shape=(pltpu.VMEM(own.shape, BF16), pltpu.VMEM(own.shape, BF16)),
+        in_specs=[INSIDE] * 3,
+        out_specs=(INSIDE, INSIDE),
+        compiler_params=room(4),
+        cost_estimate=pl.CostEstimate(flops=2 * own.size, transcendentals=0, bytes_accessed=12 * own.size),
+        name="rounded",
+    )(own, other, after)
 
 
 def total_of(parts, copies):
@@ -185,14 +186,14 @@
     )(image, own, other)
 
 
-def recover(inc, sizes, amp, loads, state, diag, phi, unroll):
+def recover(inc, sizes, amp, loads, state, diag, phi, unroll, some):
     load_cols = loads.shape[0]
     tiles = phi.shape[0]
     subs = sizes.shape[0]
-    peers, _, frows = amp.shape
-    per = frows // BLOCK
-    blocks = peers * per
+    per = amp.shape[2] // BLOCK
+    blocks = amp.shape[0] * per
     parts = tiles // unroll
+    pieces = tiles // some
     contract = (((1,), (1,)), ((), ()))
 
     def kernel(inc_hbm, sizes_hbm, amp_ref, loads_ref, state_ref, diag_ref, phi_ref, adj_hbm, sens_ref, *scratch):
@@ -208,7 +209,7 @@
         sizes_copy.wait()
 
         def adj_copy(p):
-            cols = pl.ds(pl.multiple_of(p * unroll * BLOCK, BLOCK), unroll * BLOCK)
+            cols = pl.ds(pl.multiple_of(p * some * BLOCK, BLOCK), some * BLOCK)
             return pltpu.make_async_copy(adj_ref.at[:, cols], adj_hbm.at[:, cols], sem.at[p])
 
         def part(p, carry):
@@ -229,13 +230,14 @@
                     adj_ref[:, cols] = response.astype(BF16)
                     total = jnp.sum(response * state_ref[:, cols].astype(F32), axis=1, keepdims=True)
                     sens = sens + jnp.where(lane == owner, total, jnp.zeros_like(sens))
-            adj_copy(p).start()
+                if (j + 2) % some == 0:
+                    adj_copy(p * (unroll // some) + j // some).start()
             return owner, end, sens
 
         start = (jnp.int32(0), sizes_ref[0], jnp.zeros((load_cols, subs), F32))
         _, _, sens = lax.fori_loop(0, parts, part, start)
         sens_ref[...] = sens * sens_scale
-        for p in range(parts):
+        for p in range(pieces):
             adj_copy(p).wait()
 
     return pl.pallas_call(
@@ -251,7 +253,7 @@
             pltpu.VMEM((blocks, load_cols, BLOCK), BF16),
             pltpu.SMEM(inc.shape, jnp.int32),
             pltpu.SMEM(sizes.shape, jnp.int32),
-            pltpu.SemaphoreType.DMA((parts,)),
+            pltpu.SemaphoreType.DMA((pieces,)),
             pltpu.SemaphoreType.DMA((2,)),
         ],
         compiler_params=room(6),
@@ -272,9 +274,10 @@
     wide = lax.axis_size(WIDE)
     frows = factor.shape[0]
     shifts = (1, 3, 2)
-    partial, loads_in, phi_in, own = condense(incidence, sizes, loads, phi, factor, wide, 8, 64)
-    other = moved(own, "c", 1)
+    partial, loads_in, phi_in = condense(incidence, sizes, loads, phi, wide, factor.shape[0], 8, 128)
+    other = moved(factor, "c", 1)
     own_loads = total_of([exchange(partial, WIDE)], 0)
+    own, other = rounded(factor, other, own_loads)
     chip_loads = [own_loads] + [moved(own_loads, "z", s) for s in shifts]
     image_part = times_factor(chip_loads, own, other, 512)
     rows = image_part.shape[0]
@@ -284,7 +287,7 @@
     amp_parts = times_transpose(image, own, other, 4, 128)
     amp_parts = [amp_parts[0]] + [moved(a, "z", -s) for a, s in zip(amp_parts[1:], shifts)]
     amp_all = exchange(total_of(amp_parts, wide), WIDE)
-    return recover(incidence, sizes, amp_all, loads_in, state, diag, phi_in, 64)
+    return recover(incidence, sizes, amp_all, loads_in, state, diag, phi_in, 128, 32)
 
 
 def solution(mesh):

time: 112 us -> 109 us (0.973)
  Pallas kernels: 16.8 us -> 14.9 us
    pallas_call x1, Pallas kernels: 6.9 us -> 4.78 us  [condense(): pl.pallas_call(kernel, out_shape=(jax.ShapeDtypeStruct((peers, load_cols,...]
  transfers between devices with their start and end apart: 7 -> 7, of which waited for: 6 -> 6; matrix products, arithmetic and copies ran while one was open for 0% -> 0% of each run, Pallas kernels for 0% -> 5%
where the time goes in v3:
time: 109 us
  blocking collectives  76.1 us (70%)
  Pallas kernels  14.9 us (14%)
  starting transfers between devices  10.1 us (9%)
  waiting for transfers between devices  7.12 us (7%)
    all_to_all x4, blocking collectives, exchange(): return lax.all_to_all(parts, axis, 0, 0, tiled=True)  76.1 us
    ppermute x7, starting transfers between devices, moved(): lax.ppermute(value, axis, [(i, (i + by) % peers) for i in range(peers)])  10.1 us
    ppermute x7, waiting for transfers between devices, moved(): lax.ppermute(value, axis, [(i, (i + by) % peers) for i in range(peers)])  7.12 us
    pallas_call x1, Pallas kernels, recover(): pl.pallas_call(kernel, out_shape=(jax.ShapeDtypeStruct(loads.shape, BF16)...  5.34 us
    pallas_call x1, Pallas kernels, condense(): pl.pallas_call(kernel, out_shape=(jax.ShapeDtypeStruct((peers, load_cols,...  4.78 us
    pallas_call x1, Pallas kernels, times_transpose(): pl.pallas_call(kernel, out_shape=[jax.ShapeDtypeStruct((group, frows), BF...  2.32 us
  transfers between devices with their start and end apart: 7, of which 6 were waited for; matrix products, arithmetic and copies ran while one was open for 0% of the time, Pallas kernels for 5%

profile of v3, /device:TPU:0, one launch (start us, length us, event | category | flops | bytes accessed | tf_op | source)
XLA Modules:
  0.0 109.1 jit_solution(925257840030783912)
XLA Ops:
  0.6 0.1 collective-permute-start.3
  0.7 0.0 copy-start
  0.7 4.8 %condense.1 = (bf16[16,32,1024]{2,1,0:T(8,128)(2,1)S(1)}, bf16[32,32768]{1,0:T(8,128)(2,1)S(1)}, bf16[256,128,128]{2,1,0:T(8,128)(2,1)S(1)}) custom-call(s32[256]{0:T(256)} %inc_hbm.3, s32[128]{0:T(128)} %sizes_hbm.3, bf16[32,32768]{1,0:T(8,128)(2,1)} %loads_hbm.1, bf16[256,128,128]{2,1,0:T(8,128)(2,1)} %phi_hbm.1), custom_call_target="tpu_custom_call" | custom-call | tf_op jit(solution)/shard_map/condense/pallas_call | solution.py:76
  5.5 24.8 %all_to_all.20.refs_0_ = bf16[16,32,1024]{2,1,0:T(8,128)(2,1)S(1)} all-to-all(bf16[16,32,1024]{2,1,0:T(8,128)(2,1)S(1)} %get-tuple-element.11), channel_id=1, replica_groups=mesh['x'=4,'y'=4,'z'=4,'c'=2] {'x','y'}, dimensions={0} | all-to-all | bytes 2097152 | tf_op jit(solution)/shard_map/all_to_all | solution.py:265
  30.3 0.1 total_of.3.after_ref.refs_0_
  30.5 4.0 %collective-permute-start.2 = (bf16[32,1024]{1,0:T(8,128)(2,1)S(1)}, bf16[32,1024]{1,0:T(8,128)(2,1)S(1)}, u32[]{:S(2)}, u32[]{:S(2)}) collective-permute-start(bf16[32,1024]{1,0:T(8,128)(2,1)S(1)} %total_of.3.after_ref.refs_0_), channel_id=1, source_target_pairs={{0,4},{2,6},{4,0},{6,2},{1,5},{3,7},{5,1},{7,3},{8,12},{10,14},{12... | collective-permute-start | bytes 196616 | tf_op jit(solution)/shard_map/ppermute | solution.py:270
  34.4 0.7 collective-permute-start.1
  35.1 1.3 %collective-permute-start = (bf16[32,1024]{1,0:T(8,128)(2,1)S(1)}, bf16[32,1024]{1,0:T(8,128)(2,1)S(1)}, u32[]{:S(2)}, u32[]{:S(2)}) collective-permute-start(bf16[32,1024]{1,0:T(8,128)(2,1)S(1)} %total_of.3.after_ref.refs_0_), channel_id=1, source_target_pairs={{0,2},{2,4},{4,6},{6,0},{1,3},{3,5},{5,7},{7,1},{8,10},{10,12},{12... | collective-permute-start | bytes 196616 | tf_op jit(solution)/shard_map/ppermute | solution.py:270
  36.5 0.0 collective-permute-done.3.other_ref
  36.5 0.0 copy-done
  36.5 0.8 rounded.1
  37.3 0.1 collective-permute-done.2.refs_3_
  37.3 1.4 %collective-permute-done.1.refs_2_ = bf16[32,1024]{1,0:T(8,128)(2,1)S(1)} collective-permute-done((bf16[32,1024]{1,0:T(8,128)(2,1)S(1)}, bf16[32,1024]{1,0:T(8,128)(2,1)S(1)}, u32[]{:S(2)}, u32[]{:S(2)}) %collective-permute-start.1) | collective-permute-done | bytes 65568 | tf_op jit(solution)/shard_map/ppermute | solution.py:270
  38.7 1.9 %collective-permute-done.refs_1_ = bf16[32,1024]{1,0:T(8,128)(2,1)S(1)} collective-permute-done((bf16[32,1024]{1,0:T(8,128)(2,1)S(1)}, bf16[32,1024]{1,0:T(8,128)(2,1)S(1)}, u32[]{:S(2)}, u32[]{:S(2)}) %collective-permute-start) | collective-permute-done | bytes 65568 | tf_op jit(solution)/shard_map/ppermute | solution.py:270
  40.6 1.3 %times_factor.1 = bf16[128,4096]{1,0:T(8,128)(2,1)S(1)} custom-call(bf16[32,1024]{1,0:T(8,128)(2,1)S(1)} %total_of.3.after_ref.refs_0_, bf16[32,1024]{1,0:T(8,128)(2,1)S(1)} %collective-permute-done.refs_1_, bf16[32,1024]{1,0:T(8,128)(2,1)S(1)} %collective-permute-done.1.refs_2_, bf16[32,1024]{1,0:T(8,128)(2,1)S(1)} %collective-permute-done.2.refs_3_, ...), custom_call_target="tpu_custom_call" | custom-call | tf_op jit(solution)/shard_map/times_factor/pallas_call | solution.py:155
  41.9 18.2 %all_to_all.21.refs_0_ = bf16[16,8,4096]{2,1,0:T(8,128)(2,1)S(1)} all-to-all(bf16[16,8,4096]{2,1,0:T(8,128)(2,1)S(1)} %bitcast.4), channel_id=1, replica_groups=mesh['x'=4,'y'=4,'z'=4,'c'=2] {'x','y'}, dimensions={0} | all-to-all | bytes 2097152 | tf_op jit(solution)/shard_map/all_to_all | solution.py:265
  60.1 0.2 total_of.4
  60.3 17.0 %all_to_all.22 = bf16[16,8,4096]{2,1,0:T(8,128)(2,1)S(1)} all-to-all(bf16[16,8,4096]{2,1,0:T(8,128)(2,1)S(1)} %total_of.4), channel_id=1, replica_groups=mesh['x'=4,'y'=4,'z'=4,'c'=2] {'x','y'}, dimensions={0} | all-to-all | bytes 2097152 | tf_op jit(solution)/shard_map/all_to_all | solution.py:265
  77.2 0.0 copy-start.1
  77.2 0.0 copy-start.2
  77.2 0.0 copy-start.3
  77.2 0.0 copy-start.4
  77.2 2.3 %times_transpose.1 = (bf16[32,1024]{1,0:T(8,128)(2,1)S(1)}, bf16[32,1024]{1,0:T(8,128)(2,1)S(1)}, bf16[32,1024]{1,0:T(8,128)(2,1)S(1)}, bf16[32,1024]{1,0:T(8,128)(2,1)S(1)}) custom-call(bf16[128,4096]{1,0:T(8,128)(2,1)S(1)} %bitcast.3, bf16[1024,2048]{1,0:T(8,128)(2,1)S(1)} %get-tuple-element.12.refs_4_.own_ref, ...), custom_call_target="tpu_custom_call" | custom-call | tf_op jit(solution)/shard_map/times_transpose/pallas_call | solution.py:179
  79.6 1.6 %collective-permute-start.4 = (bf16[32,1024]{1,0:T(8,128)(2,1)S(1)}, bf16[32,1024]{1,0:T(8,128)(2,1)S(1)}, u32[]{:S(2)}, u32[]{:S(2)}) collective-permute-start(bf16[32,1024]{1,0:T(8,128)(2,1)S(1)} %get-tuple-element.15), channel_id=1, source_target_pairs={{0,6},{2,0},{4,2},{6,4},{1,7},{3,1},{5,3},{7,5},{8,14},{10,8},{12,... | collective-permute-start | bytes 196616 | tf_op jit(solution)/shard_map/ppermute | solution.py:270
  81.2 0.5 collective-permute-start.5
  81.7 2.0 %collective-permute-start.6 = (bf16[32,1024]{1,0:T(8,128)(2,1)S(1)}, bf16[32,1024]{1,0:T(8,128)(2,1)S(1)}, u32[]{:S(2)}, u32[]{:S(2)}) collective-permute-start(bf16[32,1024]{1,0:T(8,128)(2,1)S(1)} %get-tuple-element.17), channel_id=1, source_target_pairs={{0,4},{2,6},{4,0},{6,2},{1,5},{3,7},{5,1},{7,3},{8,12},{10,14},{12... | collective-permute-start | bytes 196616 | tf_op jit(solution)/shard_map/ppermute | solution.py:270
  83.7 0.3 collective-permute-done.4.refs_1_
  83.9 2.8 %collective-permute-done.5.refs_2_ = bf16[32,1024]{1,0:T(8,128)(2,1)S(1)} collective-permute-done((bf16[32,1024]{1,0:T(8,128)(2,1)S(1)}, bf16[32,1024]{1,0:T(8,128)(2,1)S(1)}, u32[]{:S(2)}, u32[]{:S(2)}) %collective-permute-start.5) | collective-permute-done | bytes 65568 | tf_op jit(solution)/shard_map/ppermute | solution.py:270
  86.7 0.8 collective-permute-done.6.refs_3_
  87.4 0.1 total_of.5
  87.5 16.2 %all_to_all.23.amp_ref = bf16[16,32,1024]{2,1,0:T(8,128)(2,1)S(1)} all-to-all(bf16[16,32,1024]{2,1,0:T(8,128)(2,1)S(1)} %total_of.5), channel_id=1, replica_groups=mesh['x'=4,'y'=4,'z'=4,'c'=2] {'x','y'}, dimensions={0} | all-to-all | bytes 2097152 | tf_op jit(solution)/shard_map/all_to_all | solution.py:265
  103.7 0.0 copy-done.1
  103.7 0.0 copy-done.2
  103.7 0.0 copy-done.3
  103.7 0.0 copy-done.4
  103.7 5.3 %recover.1 = (bf16[32,32768]{1,0:T(8,128)(2,1)}, f32[32,128]{1,0:T(8,128)}) custom-call(s32[256]{0:T(256)S(1)} %copy-done.3, s32[128]{0:T(128)S(1)} %copy-done.4, bf16[16,32,1024]{2,1,0:T(8,128)(2,1)S(1)} %all_to_all.23.amp_ref, bf16[32,32768]{1,0:T(8,128)(2,1)S(1)} %get-tuple-element.18.loads_ref, bf16[32,32768]{1,0:T(8,128)(2,1)S(1)} %copy-done.1, ...), custom_call_target="tpu_custom_call" | custom-call | tf_op jit(solution)/shard_map/recover/pallas_call | solution.py:243
Async XLA Ops:
  0.6 35.8 %collective-permute-start.3 = (f32[1024,2048]{1,0:T(8,128)}, f32[1024,2048]{1,0:T(8,128)S(1)}, u32[]{:S(2)}, u32[]{:S(2)}) collective-permute-start(f32[1024,2048]{1,0:T(8,128)} %own_ref.1), channel_id=1, source_target_pairs={{0,1},{1,0},{2,3},{3,2},{4,5},{5,4},{6,7},{7,6},{8,9},{9,8},{10,11... | collective-permute-start | bytes 25165832 | tf_op jit(solution)/shard_map/ppermute | solution.py:270
  0.7 35.7 %copy-start = (f32[1024,2048]{1,0:T(8,128)S(1)}, f32[1024,2048]{1,0:T(8,128)}, u32[]{:S(2)}) copy-start(f32[1024,2048]{1,0:T(8,128)} %own_ref.1) | copy-start | bytes 25165828
  30.5 6.9 %collective-permute-start.2 = (bf16[32,1024]{1,0:T(8,128)(2,1)S(1)}, bf16[32,1024]{1,0:T(8,128)(2,1)S(1)}, u32[]{:S(2)}, u32[]{:S(2)}) collective-permute-start(bf16[32,1024]{1,0:T(8,128)(2,1)S(1)} %total_of.3.after_ref.refs_0_), channel_id=1, source_target_pairs={{0,4},{2,6},{4,0},{6,2},{1,5},{3,7},{5,1},{7,3},{8,12},{10,14},{12... | collective-permute-start | bytes 196616 | tf_op jit(solution)/shard_map/ppermute | solution.py:270
  34.4 4.3 %collective-permute-start.1 = (bf16[32,1024]{1,0:T(8,128)(2,1)S(1)}, bf16[32,1024]{1,0:T(8,128)(2,1)S(1)}, u32[]{:S(2)}, u32[]{:S(2)}) collective-permute-start(bf16[32,1024]{1,0:T(8,128)(2,1)S(1)} %total_of.3.after_ref.refs_0_), channel_id=1, source_target_pairs={{0,6},{2,0},{4,2},{6,4},{1,7},{3,1},{5,3},{7,5},{8,14},{10,8},{12,... | collective-permute-start | bytes 196616 | tf_op jit(solution)/shard_map/ppermute | solution.py:270
  35.1 5.5 %collective-permute-start = (bf16[32,1024]{1,0:T(8,128)(2,1)S(1)}, bf16[32,1024]{1,0:T(8,128)(2,1)S(1)}, u32[]{:S(2)}, u32[]{:S(2)}) collective-permute-start(bf16[32,1024]{1,0:T(8,128)(2,1)S(1)} %total_of.3.after_ref.refs_0_), channel_id=1, source_target_pairs={{0,2},{2,4},{4,6},{6,0},{1,3},{3,5},{5,7},{7,1},{8,10},{10,12},{12... | collective-permute-start | bytes 196616 | tf_op jit(solution)/shard_map/ppermute | solution.py:270
  77.2 26.5 %copy-start.1 = (bf16[32,32768]{1,0:T(8,128)(2,1)S(1)}, bf16[32,32768]{1,0:T(8,128)(2,1)}, u32[]{:S(2)}) copy-start(bf16[32,32768]{1,0:T(8,128)(2,1)} %state_ref.1) | copy-start | bytes 6291460
  77.2 26.5 %copy-start.2 = (f32[32768]{0:T(1024)S(1)}, f32[32768]{0:T(1024)}, u32[]{:S(2)}) copy-start(f32[32768]{0:T(1024)} %param.9) | copy-start | bytes 393220
  77.2 26.5 %copy-start.3 = (s32[256]{0:T(256)S(1)}, s32[256]{0:T(256)}, u32[]{:S(2)}) copy-start(s32[256]{0:T(256)} %inc_hbm.3) | copy-start | bytes 3076
  77.2 26.5 %copy-start.4 = (s32[128]{0:T(128)S(1)}, s32[128]{0:T(128)}, u32[]{:S(2)}) copy-start(s32[128]{0:T(128)} %sizes_hbm.3) | copy-start | bytes 1540
  79.6 4.3 %collective-permute-start.4 = (bf16[32,1024]{1,0:T(8,128)(2,1)S(1)}, bf16[32,1024]{1,0:T(8,128)(2,1)S(1)}, u32[]{:S(2)}, u32[]{:S(2)}) collective-permute-start(bf16[32,1024]{1,0:T(8,128)(2,1)S(1)} %get-tuple-element.15), channel_id=1, source_target_pairs={{0,6},{2,0},{4,2},{6,4},{1,7},{3,1},{5,3},{7,5},{8,14},{10,8},{12,... | collective-permute-start | bytes 196616 | tf_op jit(solution)/shard_map/ppermute | solution.py:270
  81.2 5.5 %collective-permute-start.5 = (bf16[32,1024]{1,0:T(8,128)(2,1)S(1)}, bf16[32,1024]{1,0:T(8,128)(2,1)S(1)}, u32[]{:S(2)}, u32[]{:S(2)}) collective-permute-start(bf16[32,1024]{1,0:T(8,128)(2,1)S(1)} %get-tuple-element.16), channel_id=1, source_target_pairs={{0,2},{2,4},{4,6},{6,0},{1,3},{3,5},{5,7},{7,1},{8,10},{10,12},{12... | collective-permute-start | bytes 196616 | tf_op jit(solution)/shard_map/ppermute | solution.py:270
  81.7 5.8 %collective-permute-start.6 = (bf16[32,1024]{1,0:T(8,128)(2,1)S(1)}, bf16[32,1024]{1,0:T(8,128)(2,1)S(1)}, u32[]{:S(2)}, u32[]{:S(2)}) collective-permute-start(bf16[32,1024]{1,0:T(8,128)(2,1)S(1)} %get-tuple-element.17), channel_id=1, source_target_pairs={{0,4},{2,6},{4,0},{6,2},{1,5},{3,7},{5,1},{7,3},{8,12},{10,14},{12... | collective-permute-start | bytes 196616 | tf_op jit(solution)/shard_map/ppermute | solution.py:270

commit v4 on v3

--- a/solution.py
+++ b/solution.py
@@ -191,22 +191,24 @@
     tiles = phi.shape[0]
     subs = sizes.shape[0]
     per = amp.shape[2] // BLOCK
-    blocks = amp.shape[0] * per
     parts = tiles // unroll
     pieces = tiles // some
     contract = (((1,), (1,)), ((), ()))
 
-    def kernel(inc_hbm, sizes_hbm, amp_ref, loads_ref, state_ref, diag_ref, phi_ref, adj_hbm, sens_ref, *scratch):
-        adj_ref, blk_ref, inc_ref, sizes_ref, sem, scalar_sem = scratch
+    def kernel(inc_hbm, sizes_hbm, amp_ref, loads_ref, state_ref, diag_ref, phi_ref, adj_hbm, sens_hbm, *scratch):
+        adj_ref, sens_ref, inc_ref, sizes_ref, sem, sens_sem, scalar_sem = scratch
         inc_copy = pltpu.make_async_copy(inc_hbm, inc_ref, scalar_sem.at[0])
         sizes_copy = pltpu.make_async_copy(sizes_hbm, sizes_ref, scalar_sem.at[1])
         inc_copy.start()
         sizes_copy.start()
-        for b in range(blocks):
-            blk_ref[b] = amp_ref[b // per, :, (b % per) * BLOCK : (b % per + 1) * BLOCK]
         lane = lax.broadcasted_iota(jnp.int32, (load_cols, subs), 1)
         inc_copy.wait()
         sizes_copy.wait()
+
+        def block(tile):
+            at = inc_ref[tile]
+            cols = pl.multiple_of(lax.rem(at, per) * BLOCK, BLOCK)
+            return amp_ref[lax.div(at, per), :, pl.ds(cols, BLOCK)]
 
         def adj_copy(p):
             cols = pl.ds(pl.multiple_of(p * some * BLOCK, BLOCK), some * BLOCK)
@@ -216,7 +218,7 @@
             owner, end, sens = carry
             for j in range(0, unroll, 2):
                 tile = p * unroll + j
-                rows = jnp.concatenate([blk_ref[inc_ref[tile]], blk_ref[inc_ref[tile + 1]]], axis=0)
+                rows = jnp.concatenate([block(tile), block(tile + 1)], axis=0)
                 both = phi_ref[pl.ds(tile, 2)].reshape(PAIR, BLOCK)
                 product = lax.dot_general(rows, both, contract, preferred_element_type=F32)
                 couplings = (product[:load_cols, :BLOCK], product[load_cols:, BLOCK:])
@@ -237,8 +239,11 @@
         start = (jnp.int32(0), sizes_ref[0], jnp.zeros((load_cols, subs), F32))
         _, _, sens = lax.fori_loop(0, parts, part, start)
         sens_ref[...] = sens * sens_scale
+        sens_copy = pltpu.make_async_copy(sens_ref, sens_hbm, sens_sem.at[0])
+        sens_copy.start()
         for p in range(pieces):
             adj_copy(p).wait()
+        sens_copy.wait()
 
     return pl.pallas_call(
         kernel,
@@ -247,13 +252,14 @@
             jax.ShapeDtypeStruct((load_cols, subs), F32),
         ),
         in_specs=[OUTSIDE] * 2 + [INSIDE] * 5,
-        out_specs=(OUTSIDE, INSIDE),
+        out_specs=(OUTSIDE, OUTSIDE),
         scratch_shapes=[
             pltpu.VMEM(loads.shape, BF16),
-            pltpu.VMEM((blocks, load_cols, BLOCK), BF16),
+            pltpu.VMEM((load_cols, subs), F32),
             pltpu.SMEM(inc.shape, jnp.int32),
             pltpu.SMEM(sizes.shape, jnp.int32),
             pltpu.SemaphoreType.DMA((pieces,)),
+            pltpu.SemaphoreType.DMA((1,)),
             pltpu.SemaphoreType.DMA((2,)),
         ],
         compiler_params=room(6),
@@ -287,7 +293,7 @@
     amp_parts = times_transpose(image, own, other, 4, 128)
     amp_parts = [amp_parts[0]] + [moved(a, "z", -s) for a, s in zip(amp_parts[1:], shifts)]
     amp_all = exchange(total_of(amp_parts, wide), WIDE)
-    return recover(incidence, sizes, amp_all, loads_in, state, diag, phi_in, 128, 32)
+    return recover(incidence, sizes, amp_all, loads_in, state, diag, phi_in, 256, 32)
 
 
 def solution(mesh):

time: 109 us -> 109 us (level)
  no operation moved by 1% of the time
where the time goes in v4:
time: 109 us; the launch traced here: 108 us
  blocking collectives  76.1 us (70%)
  Pallas kernels  14 us (13%)
  starting transfers between devices  10.2 us (9%)
  waiting for transfers between devices  7.11 us (7%)
    all_to_all x4, blocking collectives, exchange(): return lax.all_to_all(parts, axis, 0, 0, tiled=True)  76.1 us
    ppermute x7, starting transfers between devices, moved(): lax.ppermute(value, axis, [(i, (i + by) % peers) for i in range(peers)])  10.2 us
    ppermute x7, waiting for transfers between devices, moved(): lax.ppermute(value, axis, [(i, (i + by) % peers) for i in range(peers)])  7.11 us
    pallas_call x1, Pallas kernels, condense(): pl.pallas_call(kernel, out_shape=(jax.ShapeDtypeStruct((peers, load_cols,...  4.78 us
    pallas_call x1, Pallas kernels, recover(): pl.pallas_call(kernel, out_shape=(jax.ShapeDtypeStruct(loads.shape, BF16)...  4.39 us
    pallas_call x1, Pallas kernels, times_transpose(): pl.pallas_call(kernel, out_shape=[jax.ShapeDtypeStruct((group, frows), BF...  2.33 us
  transfers between devices with their start and end apart: 7, of which 6 were waited for; matrix products, arithmetic and copies ran while one was open for 0% of the time, Pallas kernels for 5%

profile of v4, /device:TPU:0, one launch (start us, length us, event | category | flops | bytes accessed | tf_op | source)
XLA Modules:
  0.0 108.3 jit_solution(7502880637260010163)
XLA Ops:
  0.6 0.1 collective-permute-start.3
  0.7 0.0 copy-start
  0.7 4.8 %condense.1 = (bf16[16,32,1024]{2,1,0:T(8,128)(2,1)S(1)}, bf16[32,32768]{1,0:T(8,128)(2,1)S(1)}, bf16[256,128,128]{2,1,0:T(8,128)(2,1)S(1)}) custom-call(s32[256]{0:T(256)} %inc_hbm.3, s32[128]{0:T(128)} %sizes_hbm.3, bf16[32,32768]{1,0:T(8,128)(2,1)} %loads_hbm.1, bf16[256,128,128]{2,1,0:T(8,128)(2,1)} %phi_hbm.1), custom_call_target="tpu_custom_call" | custom-call | tf_op jit(solution)/shard_map/condense/pallas_call | solution.py:76
  5.5 24.8 %all_to_all.20.refs_0_ = bf16[16,32,1024]{2,1,0:T(8,128)(2,1)S(1)} all-to-all(bf16[16,32,1024]{2,1,0:T(8,128)(2,1)S(1)} %get-tuple-element.11), channel_id=1, replica_groups=mesh['x'=4,'y'=4,'z'=4,'c'=2] {'x','y'}, dimensions={0} | all-to-all | bytes 2097152 | tf_op jit(solution)/shard_map/all_to_all | solution.py:271
  30.3 0.1 total_of.3.after_ref.refs_0_
  30.5 4.0 %collective-permute-start.2 = (bf16[32,1024]{1,0:T(8,128)(2,1)S(1)}, bf16[32,1024]{1,0:T(8,128)(2,1)S(1)}, u32[]{:S(2)}, u32[]{:S(2)}) collective-permute-start(bf16[32,1024]{1,0:T(8,128)(2,1)S(1)} %total_of.3.after_ref.refs_0_), channel_id=1, source_target_pairs={{0,4},{2,6},{4,0},{6,2},{1,5},{3,7},{5,1},{7,3},{8,12},{10,14},{12... | collective-permute-start | bytes 196616 | tf_op jit(solution)/shard_map/ppermute | solution.py:276
  34.4 0.7 collective-permute-start.1
  35.1 1.3 %collective-permute-start = (bf16[32,1024]{1,0:T(8,128)(2,1)S(1)}, bf16[32,1024]{1,0:T(8,128)(2,1)S(1)}, u32[]{:S(2)}, u32[]{:S(2)}) collective-permute-start(bf16[32,1024]{1,0:T(8,128)(2,1)S(1)} %total_of.3.after_ref.refs_0_), channel_id=1, source_target_pairs={{0,2},{2,4},{4,6},{6,0},{1,3},{3,5},{5,7},{7,1},{8,10},{10,12},{12... | collective-permute-start | bytes 196616 | tf_op jit(solution)/shard_map/ppermute | solution.py:276
  36.5 0.0 collective-permute-done.3.other_ref
  36.5 0.0 copy-done
  36.5 0.8 rounded.1
  37.3 0.1 collective-permute-done.2.refs_3_
  37.3 1.4 %collective-permute-done.1.refs_2_ = bf16[32,1024]{1,0:T(8,128)(2,1)S(1)} collective-permute-done((bf16[32,1024]{1,0:T(8,128)(2,1)S(1)}, bf16[32,1024]{1,0:T(8,128)(2,1)S(1)}, u32[]{:S(2)}, u32[]{:S(2)}) %collective-permute-start.1) | collective-permute-done | bytes 65568 | tf_op jit(solution)/shard_map/ppermute | solution.py:276
  38.7 1.9 %collective-permute-done.refs_1_ = bf16[32,1024]{1,0:T(8,128)(2,1)S(1)} collective-permute-done((bf16[32,1024]{1,0:T(8,128)(2,1)S(1)}, bf16[32,1024]{1,0:T(8,128)(2,1)S(1)}, u32[]{:S(2)}, u32[]{:S(2)}) %collective-permute-start) | collective-permute-done | bytes 65568 | tf_op jit(solution)/shard_map/ppermute | solution.py:276
  40.6 1.3 %times_factor.1 = bf16[128,4096]{1,0:T(8,128)(2,1)S(1)} custom-call(bf16[32,1024]{1,0:T(8,128)(2,1)S(1)} %total_of.3.after_ref.refs_0_, bf16[32,1024]{1,0:T(8,128)(2,1)S(1)} %collective-permute-done.refs_1_, bf16[32,1024]{1,0:T(8,128)(2,1)S(1)} %collective-permute-done.1.refs_2_, bf16[32,1024]{1,0:T(8,128)(2,1)S(1)} %collective-permute-done.2.refs_3_, ...), custom_call_target="tpu_custom_call" | custom-call | tf_op jit(solution)/shard_map/times_factor/pallas_call | solution.py:155
  41.9 18.2 %all_to_all.21.refs_0_ = bf16[16,8,4096]{2,1,0:T(8,128)(2,1)S(1)} all-to-all(bf16[16,8,4096]{2,1,0:T(8,128)(2,1)S(1)} %bitcast.4), channel_id=1, replica_groups=mesh['x'=4,'y'=4,'z'=4,'c'=2] {'x','y'}, dimensions={0} | all-to-all | bytes 2097152 | tf_op jit(solution)/shard_map/all_to_all | solution.py:271
  60.1 0.2 total_of.4
  60.3 17.0 %all_to_all.22 = bf16[16,8,4096]{2,1,0:T(8,128)(2,1)S(1)} all-to-all(bf16[16,8,4096]{2,1,0:T(8,128)(2,1)S(1)} %total_of.4), channel_id=1, replica_groups=mesh['x'=4,'y'=4,'z'=4,'c'=2] {'x','y'}, dimensions={0} | all-to-all | bytes 2097152 | tf_op jit(solution)/shard_map/all_to_all | solution.py:271
  77.2 0.0 copy-start.1
  77.2 0.0 copy-start.2
  77.2 0.0 copy-start.3
  77.2 0.0 copy-start.4
  77.2 2.3 %times_transpose.1 = (bf16[32,1024]{1,0:T(8,128)(2,1)S(1)}, bf16[32,1024]{1,0:T(8,128)(2,1)S(1)}, bf16[32,1024]{1,0:T(8,128)(2,1)S(1)}, bf16[32,1024]{1,0:T(8,128)(2,1)S(1)}) custom-call(bf16[128,4096]{1,0:T(8,128)(2,1)S(1)} %bitcast.3, bf16[1024,2048]{1,0:T(8,128)(2,1)S(1)} %get-tuple-element.12.refs_4_.own_ref, ...), custom_call_target="tpu_custom_call" | custom-call | tf_op jit(solution)/shard_map/times_transpose/pallas_call | solution.py:179
  79.6 1.6 %collective-permute-start.4 = (bf16[32,1024]{1,0:T(8,128)(2,1)S(1)}, bf16[32,1024]{1,0:T(8,128)(2,1)S(1)}, u32[]{:S(2)}, u32[]{:S(2)}) collective-permute-start(bf16[32,1024]{1,0:T(8,128)(2,1)S(1)} %get-tuple-element.15), channel_id=1, source_target_pairs={{0,6},{2,0},{4,2},{6,4},{1,7},{3,1},{5,3},{7,5},{8,14},{10,8},{12,... | collective-permute-start | bytes 196616 | tf_op jit(solution)/shard_map/ppermute | solution.py:276
  81.2 0.5 collective-permute-start.5
  81.7 2.0 %collective-permute-start.6 = (bf16[32,1024]{1,0:T(8,128)(2,1)S(1)}, bf16[32,1024]{1,0:T(8,128)(2,1)S(1)}, u32[]{:S(2)}, u32[]{:S(2)}) collective-permute-start(bf16[32,1024]{1,0:T(8,128)(2,1)S(1)} %get-tuple-element.17), channel_id=1, source_target_pairs={{0,4},{2,6},{4,0},{6,2},{1,5},{3,7},{5,1},{7,3},{8,12},{10,14},{12... | collective-permute-start | bytes 196616 | tf_op jit(solution)/shard_map/ppermute | solution.py:276
  83.7 0.2 collective-permute-done.4.refs_1_
  83.9 2.8 %collective-permute-done.5.refs_2_ = bf16[32,1024]{1,0:T(8,128)(2,1)S(1)} collective-permute-done((bf16[32,1024]{1,0:T(8,128)(2,1)S(1)}, bf16[32,1024]{1,0:T(8,128)(2,1)S(1)}, u32[]{:S(2)}, u32[]{:S(2)}) %collective-permute-start.5) | collective-permute-done | bytes 65568 | tf_op jit(solution)/shard_map/ppermute | solution.py:276
  86.7 0.8 collective-permute-done.6.refs_3_
  87.4 0.1 total_of.5
  87.6 16.2 %all_to_all.23.amp_ref = bf16[16,32,1024]{2,1,0:T(8,128)(2,1)S(1)} all-to-all(bf16[16,32,1024]{2,1,0:T(8,128)(2,1)S(1)} %total_of.5), channel_id=1, replica_groups=mesh['x'=4,'y'=4,'z'=4,'c'=2] {'x','y'}, dimensions={0} | all-to-all | bytes 2097152 | tf_op jit(solution)/shard_map/all_to_all | solution.py:271
  103.7 0.0 copy-done.1
  103.7 0.0 copy-done.2
  103.7 0.0 copy-done.3
  103.7 0.0 copy-done.4
  103.7 4.4 %recover.1 = (bf16[32,32768]{1,0:T(8,128)(2,1)}, f32[32,128]{1,0:T(8,128)}) custom-call(s32[256]{0:T(256)S(1)} %copy-done.3, s32[128]{0:T(128)S(1)} %copy-done.4, bf16[16,32,1024]{2,1,0:T(8,128)(2,1)S(1)} %all_to_all.23.amp_ref, bf16[32,32768]{1,0:T(8,128)(2,1)S(1)} %get-tuple-element.18.loads_ref, bf16[32,32768]{1,0:T(8,128)(2,1)S(1)} %copy-done.1, ...), custom_call_target="tpu_custom_call" | custom-call | tf_op jit(solution)/shard_map/recover/pallas_call | solution.py:248
Async XLA Ops:
  0.6 35.8 %collective-permute-start.3 = (f32[1024,2048]{1,0:T(8,128)}, f32[1024,2048]{1,0:T(8,128)S(1)}, u32[]{:S(2)}, u32[]{:S(2)}) collective-permute-start(f32[1024,2048]{1,0:T(8,128)} %own_ref.1), channel_id=1, source_target_pairs={{0,1},{1,0},{2,3},{3,2},{4,5},{5,4},{6,7},{7,6},{8,9},{9,8},{10,11... | collective-permute-start | bytes 25165832 | tf_op jit(solution)/shard_map/ppermute | solution.py:276
  0.7 35.7 %copy-start = (f32[1024,2048]{1,0:T(8,128)S(1)}, f32[1024,2048]{1,0:T(8,128)}, u32[]{:S(2)}) copy-start(f32[1024,2048]{1,0:T(8,128)} %own_ref.1) | copy-start | bytes 25165828
  30.5 6.9 %collective-permute-start.2 = (bf16[32,1024]{1,0:T(8,128)(2,1)S(1)}, bf16[32,1024]{1,0:T(8,128)(2,1)S(1)}, u32[]{:S(2)}, u32[]{:S(2)}) collective-permute-start(bf16[32,1024]{1,0:T(8,128)(2,1)S(1)} %total_of.3.after_ref.refs_0_), channel_id=1, source_target_pairs={{0,4},{2,6},{4,0},{6,2},{1,5},{3,7},{5,1},{7,3},{8,12},{10,14},{12... | collective-permute-start | bytes 196616 | tf_op jit(solution)/shard_map/ppermute | solution.py:276
  34.4 4.3 %collective-permute-start.1 = (bf16[32,1024]{1,0:T(8,128)(2,1)S(1)}, bf16[32,1024]{1,0:T(8,128)(2,1)S(1)}, u32[]{:S(2)}, u32[]{:S(2)}) collective-permute-start(bf16[32,1024]{1,0:T(8,128)(2,1)S(1)} %total_of.3.after_ref.refs_0_), channel_id=1, source_target_pairs={{0,6},{2,0},{4,2},{6,4},{1,7},{3,1},{5,3},{7,5},{8,14},{10,8},{12,... | collective-permute-start | bytes 196616 | tf_op jit(solution)/shard_map/ppermute | solution.py:276
  35.1 5.5 %collective-permute-start = (bf16[32,1024]{1,0:T(8,128)(2,1)S(1)}, bf16[32,1024]{1,0:T(8,128)(2,1)S(1)}, u32[]{:S(2)}, u32[]{:S(2)}) collective-permute-start(bf16[32,1024]{1,0:T(8,128)(2,1)S(1)} %total_of.3.after_ref.refs_0_), channel_id=1, source_target_pairs={{0,2},{2,4},{4,6},{6,0},{1,3},{3,5},{5,7},{7,1},{8,10},{10,12},{12... | collective-permute-start | bytes 196616 | tf_op jit(solution)/shard_map/ppermute | solution.py:276
  77.2 26.5 %copy-start.1 = (bf16[32,32768]{1,0:T(8,128)(2,1)S(1)}, bf16[32,32768]{1,0:T(8,128)(2,1)}, u32[]{:S(2)}) copy-start(bf16[32,32768]{1,0:T(8,128)(2,1)} %state_ref.1) | copy-start | bytes 6291460
  77.2 26.5 %copy-start.2 = (f32[32768]{0:T(1024)S(1)}, f32[32768]{0:T(1024)}, u32[]{:S(2)}) copy-start(f32[32768]{0:T(1024)} %param.9) | copy-start | bytes 393220
  77.2 26.5 %copy-start.3 = (s32[256]{0:T(256)S(1)}, s32[256]{0:T(256)}, u32[]{:S(2)}) copy-start(s32[256]{0:T(256)} %inc_hbm.3) | copy-start | bytes 3076
  77.2 26.5 %copy-start.4 = (s32[128]{0:T(128)S(1)}, s32[128]{0:T(128)}, u32[]{:S(2)}) copy-start(s32[128]{0:T(128)} %sizes_hbm.3) | copy-start | bytes 1540
  79.6 4.3 %collective-permute-start.4 = (bf16[32,1024]{1,0:T(8,128)(2,1)S(1)}, bf16[32,1024]{1,0:T(8,128)(2,1)S(1)}, u32[]{:S(2)}, u32[]{:S(2)}) collective-permute-start(bf16[32,1024]{1,0:T(8,128)(2,1)S(1)} %get-tuple-element.15), channel_id=1, source_target_pairs={{0,6},{2,0},{4,2},{6,4},{1,7},{3,1},{5,3},{7,5},{8,14},{10,8},{12,... | collective-permute-start | bytes 196616 | tf_op jit(solution)/shard_map/ppermute | solution.py:276
  81.2 5.5 %collective-permute-start.5 = (bf16[32,1024]{1,0:T(8,128)(2,1)S(1)}, bf16[32,1024]{1,0:T(8,128)(2,1)S(1)}, u32[]{:S(2)}, u32[]{:S(2)}) collective-permute-start(bf16[32,1024]{1,0:T(8,128)(2,1)S(1)} %get-tuple-element.16), channel_id=1, source_target_pairs={{0,2},{2,4},{4,6},{6,0},{1,3},{3,5},{5,7},{7,1},{8,10},{10,12},{12... | collective-permute-start | bytes 196616 | tf_op jit(solution)/shard_map/ppermute | solution.py:276
  81.7 5.8 %collective-permute-start.6 = (bf16[32,1024]{1,0:T(8,128)(2,1)S(1)}, bf16[32,1024]{1,0:T(8,128)(2,1)S(1)}, u32[]{:S(2)}, u32[]{:S(2)}) collective-permute-start(bf16[32,1024]{1,0:T(8,128)(2,1)S(1)} %get-tuple-element.17), channel_id=1, source_target_pairs={{0,4},{2,6},{4,0},{6,2},{1,5},{3,7},{5,1},{7,3},{8,12},{10,14},{12... | collective-permute-start | bytes 196616 | tf_op jit(solution)/shard_map/ppermute | solution.py:276

commit v5 on v4

--- a/solution.py
+++ b/solution.py
@@ -276,22 +276,26 @@
     return lax.ppermute(value, axis, [(i, (i + by) % peers) for i in range(peers)])
 
 
+def swapped(value, axis, bits):
+    return lax.ppermute(value, axis, [(i, i ^ bits) for i in range(lax.axis_size(axis))])
+
+
 def body(loads, state, modal_diag, phi, incidence, sizes, factor):
     wide = lax.axis_size(WIDE)
     frows = factor.shape[0]
-    shifts = (1, 3, 2)
+    others = (1, 3, 2)
     partial, loads_in, phi_in = condense(incidence, sizes, loads, phi, wide, factor.shape[0], 8, 128)
     other = moved(factor, "c", 1)
     own_loads = total_of([exchange(partial, WIDE)], 0)
     own, other = rounded(factor, other, own_loads)
-    chip_loads = [own_loads] + [moved(own_loads, "z", s) for s in shifts]
+    chip_loads = [own_loads] + [swapped(own_loads, "z", b) for b in others]
     image_part = times_factor(chip_loads, own, other, 512)
     rows = image_part.shape[0]
     image_parts = exchange(image_part.reshape(wide, rows // wide, -1), WIDE)
     image = exchange(total_of([image_parts], wide), WIDE).reshape(rows, -1)
     diag = modal_diag.reshape(-1, BLOCK)
     amp_parts = times_transpose(image, own, other, 4, 128)
-    amp_parts = [amp_parts[0]] + [moved(a, "z", -s) for a, s in zip(amp_parts[1:], shifts)]
+    amp_parts = [amp_parts[0]] + [swapped(a, "z", b) for a, b in reversed(list(zip(amp_parts[1:], others)))]
     amp_all = exchange(total_of(amp_parts, wide), WIDE)
     return recover(incidence, sizes, amp_all, loads_in, state, diag, phi_in, 256, 32)
 

time: 109 us -> 109 us (level)
  starting transfers between devices: 10.2 us -> 9.08 us
    ppermute x7 -> x1, starting transfers between devices: 10.2 us -> 0.08 us  [moved(): lax.ppermute(value, axis, [(i, (i + by) % peers) for i in range(peers)])]
    ppermute x0 -> x6, starting transfers between devices: none -> 9 us  [swapped(): lax.ppermute(value, axis, [(i, i ^ bits) for i in range(lax.axis_size(axi...]
    ppermute x0 -> x6, waiting for transfers between devices: none -> 7.9 us  [swapped(): lax.ppermute(value, axis, [(i, i ^ bits) for i in range(lax.axis_size(axi...]
    ppermute x7 -> x1, waiting for transfers between devices: 7.11 us -> 0.01 us  [moved(): lax.ppermute(value, axis, [(i, (i + by) % peers) for i in range(peers)])]
  transfers between devices with their start and end apart: 7 -> 7, of which waited for: 6 -> 5; matrix products, arithmetic and copies ran while one was open for 0% -> 0% of each run, Pallas kernels for 5% -> 5%
where the time goes in v5:
time: 109 us; the launch traced here: 108 us
  blocking collectives  76.7 us (70%)
  Pallas kernels  14 us (13%)
  starting transfers between devices  9.08 us (8%)
  waiting for transfers between devices  7.9 us (7%)
    all_to_all x4, blocking collectives, exchange(): return lax.all_to_all(parts, axis, 0, 0, tiled=True)  76.7 us
    ppermute x6, starting transfers between devices, swapped(): lax.ppermute(value, axis, [(i, i ^ bits) for i in range(lax.axis_size(axi...  9 us
    ppermute x6, waiting for transfers between devices, swapped(): lax.ppermute(value, axis, [(i, i ^ bits) for i in range(lax.axis_size(axi...  7.9 us
    pallas_call x1, Pallas kernels, condense(): pl.pallas_call(kernel, out_shape=(jax.ShapeDtypeStruct((peers, load_cols,...  4.78 us
    pallas_call x1, Pallas kernels, recover(): pl.pallas_call(kernel, out_shape=(jax.ShapeDtypeStruct(loads.shape, BF16)...  4.38 us
    pallas_call x1, Pallas kernels, times_transpose(): pl.pallas_call(kernel, out_shape=[jax.ShapeDtypeStruct((group, frows), BF...  2.33 us
  transfers between devices with their start and end apart: 7, of which 5 were waited for; matrix products, arithmetic and copies ran while one was open for 0% of the time, Pallas kernels for 5%

profile of v5, /device:TPU:0, one launch (start us, length us, event | category | flops | bytes accessed | tf_op | source)
XLA Modules:
  0.0 108.4 jit_solution(14361970716219141747)
XLA Ops:
  0.6 0.1 collective-permute-start.3
  0.7 0.0 copy-start
  0.7 4.8 %condense.1 = (bf16[16,32,1024]{2,1,0:T(8,128)(2,1)S(1)}, bf16[32,32768]{1,0:T(8,128)(2,1)S(1)}, bf16[256,128,128]{2,1,0:T(8,128)(2,1)S(1)}) custom-call(s32[256]{0:T(256)} %inc_hbm.3, s32[128]{0:T(128)} %sizes_hbm.3, bf16[32,32768]{1,0:T(8,128)(2,1)} %loads_hbm.1, bf16[256,128,128]{2,1,0:T(8,128)(2,1)} %phi_hbm.1), custom_call_target="tpu_custom_call" | custom-call | tf_op jit(solution)/shard_map/condense/pallas_call | solution.py:76
  5.5 24.8 %all_to_all.20.refs_0_ = bf16[16,32,1024]{2,1,0:T(8,128)(2,1)S(1)} all-to-all(bf16[16,32,1024]{2,1,0:T(8,128)(2,1)S(1)} %get-tuple-element.11), channel_id=1, replica_groups=mesh['x'=4,'y'=4,'z'=4,'c'=2] {'x','y'}, dimensions={0} | all-to-all | bytes 2097152 | tf_op jit(solution)/shard_map/all_to_all | solution.py:271
  30.3 0.1 total_of.3.after_ref.refs_0_
  30.5 4.0 %collective-permute-start.2 = (bf16[32,1024]{1,0:T(8,128)(2,1)S(1)}, bf16[32,1024]{1,0:T(8,128)(2,1)S(1)}, u32[]{:S(2)}, u32[]{:S(2)}) collective-permute-start(bf16[32,1024]{1,0:T(8,128)(2,1)S(1)} %total_of.3.after_ref.refs_0_), channel_id=1, source_target_pairs={{0,4},{2,6},{4,0},{6,2},{1,5},{3,7},{5,1},{7,3},{8,12},{10,14},{12... | collective-permute-start | bytes 196616 | tf_op jit(solution)/shard_map/ppermute | solution.py:280
  34.4 0.7 collective-permute-start.1
  35.1 0.3 collective-permute-start
  35.5 0.0 collective-permute-done.3.other_ref
  35.5 0.0 copy-done
  35.5 0.8 rounded.1
  36.3 0.5 collective-permute-done.2.refs_3_
  36.7 3.2 %collective-permute-done.1.refs_2_ = bf16[32,1024]{1,0:T(8,128)(2,1)S(1)} collective-permute-done((bf16[32,1024]{1,0:T(8,128)(2,1)S(1)}, bf16[32,1024]{1,0:T(8,128)(2,1)S(1)}, u32[]{:S(2)}, u32[]{:S(2)}) %collective-permute-start.1) | collective-permute-done | bytes 65568 | tf_op jit(solution)/shard_map/ppermute | solution.py:280
  39.9 0.0 collective-permute-done.refs_1_
  39.9 1.3 %times_factor.1 = bf16[128,4096]{1,0:T(8,128)(2,1)S(1)} custom-call(bf16[32,1024]{1,0:T(8,128)(2,1)S(1)} %total_of.3.after_ref.refs_0_, bf16[32,1024]{1,0:T(8,128)(2,1)S(1)} %collective-permute-done.refs_1_, bf16[32,1024]{1,0:T(8,128)(2,1)S(1)} %collective-permute-done.1.refs_2_, bf16[32,1024]{1,0:T(8,128)(2,1)S(1)} %collective-permute-done.2.refs_3_, ...), custom_call_target="tpu_custom_call" | custom-call | tf_op jit(solution)/shard_map/times_factor/pallas_call | solution.py:155
  41.2 18.5 %all_to_all.21.refs_0_ = bf16[16,8,4096]{2,1,0:T(8,128)(2,1)S(1)} all-to-all(bf16[16,8,4096]{2,1,0:T(8,128)(2,1)S(1)} %bitcast.4), channel_id=1, replica_groups=mesh['x'=4,'y'=4,'z'=4,'c'=2] {'x','y'}, dimensions={0} | all-to-all | bytes 2097152 | tf_op jit(solution)/shard_map/all_to_all | solution.py:271
  59.7 0.2 total_of.4
  59.8 17.3 %all_to_all.22 = bf16[16,8,4096]{2,1,0:T(8,128)(2,1)S(1)} all-to-all(bf16[16,8,4096]{2,1,0:T(8,128)(2,1)S(1)} %total_of.4), channel_id=1, replica_groups=mesh['x'=4,'y'=4,'z'=4,'c'=2] {'x','y'}, dimensions={0} | all-to-all | bytes 2097152 | tf_op jit(solution)/shard_map/all_to_all | solution.py:271
  77.1 0.0 copy-start.1
  77.1 0.0 copy-start.2
  77.1 0.0 copy-start.3
  77.1 0.0 copy-start.4
  77.1 2.3 %times_transpose.1 = (bf16[32,1024]{1,0:T(8,128)(2,1)S(1)}, bf16[32,1024]{1,0:T(8,128)(2,1)S(1)}, bf16[32,1024]{1,0:T(8,128)(2,1)S(1)}, bf16[32,1024]{1,0:T(8,128)(2,1)S(1)}) custom-call(bf16[128,4096]{1,0:T(8,128)(2,1)S(1)} %bitcast.3, bf16[1024,2048]{1,0:T(8,128)(2,1)S(1)} %get-tuple-element.12.refs_4_.own_ref, ...), custom_call_target="tpu_custom_call" | custom-call | tf_op jit(solution)/shard_map/times_transpose/pallas_call | solution.py:179
  79.5 2.0 %collective-permute-start.4 = (bf16[32,1024]{1,0:T(8,128)(2,1)S(1)}, bf16[32,1024]{1,0:T(8,128)(2,1)S(1)}, u32[]{:S(2)}, u32[]{:S(2)}) collective-permute-start(bf16[32,1024]{1,0:T(8,128)(2,1)S(1)} %get-tuple-element.15), channel_id=1, source_target_pairs={{0,4},{2,6},{4,0},{6,2},{1,5},{3,7},{5,1},{7,3},{8,12},{10,14},{12... | collective-permute-start | bytes 196616 | tf_op jit(solution)/shard_map/ppermute | solution.py:280
  81.4 2.0 %collective-permute-start.5 = (bf16[32,1024]{1,0:T(8,128)(2,1)S(1)}, bf16[32,1024]{1,0:T(8,128)(2,1)S(1)}, u32[]{:S(2)}, u32[]{:S(2)}) collective-permute-start(bf16[32,1024]{1,0:T(8,128)(2,1)S(1)} %get-tuple-element.16), channel_id=1, source_target_pairs={{0,6},{2,4},{4,2},{6,0},{1,7},{3,5},{5,3},{7,1},{8,14},{10,12},{12... | collective-permute-start | bytes 196616 | tf_op jit(solution)/shard_map/ppermute | solution.py:280
  83.5 0.0 collective-permute-start.6
  83.5 1.8 %collective-permute-done.4.refs_1_ = bf16[32,1024]{1,0:T(8,128)(2,1)S(1)} collective-permute-done((bf16[32,1024]{1,0:T(8,128)(2,1)S(1)}, bf16[32,1024]{1,0:T(8,128)(2,1)S(1)}, u32[]{:S(2)}, u32[]{:S(2)}) %collective-permute-start.4) | collective-permute-done | bytes 65568 | tf_op jit(solution)/shard_map/ppermute | solution.py:280
  85.3 1.6 %collective-permute-done.5.refs_2_ = bf16[32,1024]{1,0:T(8,128)(2,1)S(1)} collective-permute-done((bf16[32,1024]{1,0:T(8,128)(2,1)S(1)}, bf16[32,1024]{1,0:T(8,128)(2,1)S(1)}, u32[]{:S(2)}, u32[]{:S(2)}) %collective-permute-start.5) | collective-permute-done | bytes 65568 | tf_op jit(solution)/shard_map/ppermute | solution.py:280
  86.9 0.8 collective-permute-done.6.refs_3_
  87.7 0.1 total_of.5
  87.9 16.2 %all_to_all.23.amp_ref = bf16[16,32,1024]{2,1,0:T(8,128)(2,1)S(1)} all-to-all(bf16[16,32,1024]{2,1,0:T(8,128)(2,1)S(1)} %total_of.5), channel_id=1, replica_groups=mesh['x'=4,'y'=4,'z'=4,'c'=2] {'x','y'}, dimensions={0} | all-to-all | bytes 2097152 | tf_op jit(solution)/shard_map/all_to_all | solution.py:271
  104.0 0.0 copy-done.1
  104.0 0.0 copy-done.2
  104.0 0.0 copy-done.3
  104.0 0.0 copy-done.4
  104.0 4.4 %recover.1 = (bf16[32,32768]{1,0:T(8,128)(2,1)}, f32[32,128]{1,0:T(8,128)}) custom-call(s32[256]{0:T(256)S(1)} %copy-done.3, s32[128]{0:T(128)S(1)} %copy-done.4, bf16[16,32,1024]{2,1,0:T(8,128)(2,1)S(1)} %all_to_all.23.amp_ref, bf16[32,32768]{1,0:T(8,128)(2,1)S(1)} %get-tuple-element.18.loads_ref, bf16[32,32768]{1,0:T(8,128)(2,1)S(1)} %copy-done.1, ...), custom_call_target="tpu_custom_call" | custom-call | tf_op jit(solution)/shard_map/recover/pallas_call | solution.py:248
Async XLA Ops:
  0.6 34.8 %collective-permute-start.3 = (f32[1024,2048]{1,0:T(8,128)}, f32[1024,2048]{1,0:T(8,128)S(1)}, u32[]{:S(2)}, u32[]{:S(2)}) collective-permute-start(f32[1024,2048]{1,0:T(8,128)} %own_ref.1), channel_id=1, source_target_pairs={{0,1},{1,0},{2,3},{3,2},{4,5},{5,4},{6,7},{7,6},{8,9},{9,8},{10,11... | collective-permute-start | bytes 25165832 | tf_op jit(solution)/shard_map/ppermute | solution.py:276
  0.7 34.7 %copy-start = (f32[1024,2048]{1,0:T(8,128)S(1)}, f32[1024,2048]{1,0:T(8,128)}, u32[]{:S(2)}) copy-start(f32[1024,2048]{1,0:T(8,128)} %own_ref.1) | copy-start | bytes 25165828
  30.5 6.3 %collective-permute-start.2 = (bf16[32,1024]{1,0:T(8,128)(2,1)S(1)}, bf16[32,1024]{1,0:T(8,128)(2,1)S(1)}, u32[]{:S(2)}, u32[]{:S(2)}) collective-permute-start(bf16[32,1024]{1,0:T(8,128)(2,1)S(1)} %total_of.3.after_ref.refs_0_), channel_id=1, source_target_pairs={{0,4},{2,6},{4,0},{6,2},{1,5},{3,7},{5,1},{7,3},{8,12},{10,14},{12... | collective-permute-start | bytes 196616 | tf_op jit(solution)/shard_map/ppermute | solution.py:280
  34.4 5.5 %collective-permute-start.1 = (bf16[32,1024]{1,0:T(8,128)(2,1)S(1)}, bf16[32,1024]{1,0:T(8,128)(2,1)S(1)}, u32[]{:S(2)}, u32[]{:S(2)}) collective-permute-start(bf16[32,1024]{1,0:T(8,128)(2,1)S(1)} %total_of.3.after_ref.refs_0_), channel_id=1, source_target_pairs={{0,6},{2,4},{4,2},{6,0},{1,7},{3,5},{5,3},{7,1},{8,14},{10,12},{12... | collective-permute-start | bytes 196616 | tf_op jit(solution)/shard_map/ppermute | solution.py:280
  35.1 4.8 %collective-permute-start = (bf16[32,1024]{1,0:T(8,128)(2,1)S(1)}, bf16[32,1024]{1,0:T(8,128)(2,1)S(1)}, u32[]{:S(2)}, u32[]{:S(2)}) collective-permute-start(bf16[32,1024]{1,0:T(8,128)(2,1)S(1)} %total_of.3.after_ref.refs_0_), channel_id=1, source_target_pairs={{0,2},{2,0},{4,6},{6,4},{1,3},{3,1},{5,7},{7,5},{8,10},{10,8},{12,... | collective-permute-start | bytes 196616 | tf_op jit(solution)/shard_map/ppermute | solution.py:280
  77.1 26.9 %copy-start.1 = (bf16[32,32768]{1,0:T(8,128)(2,1)S(1)}, bf16[32,32768]{1,0:T(8,128)(2,1)}, u32[]{:S(2)}) copy-start(bf16[32,32768]{1,0:T(8,128)(2,1)} %state_ref.1) | copy-start | bytes 6291460
  77.1 26.9 %copy-start.2 = (f32[32768]{0:T(1024)S(1)}, f32[32768]{0:T(1024)}, u32[]{:S(2)}) copy-start(f32[32768]{0:T(1024)} %param.9) | copy-start | bytes 393220
  77.1 26.9 %copy-start.3 = (s32[256]{0:T(256)S(1)}, s32[256]{0:T(256)}, u32[]{:S(2)}) copy-start(s32[256]{0:T(256)} %inc_hbm.3) | copy-start | bytes 3076
  77.1 26.9 %copy-start.4 = (s32[128]{0:T(128)S(1)}, s32[128]{0:T(128)}, u32[]{:S(2)}) copy-start(s32[128]{0:T(128)} %sizes_hbm.3) | copy-start | bytes 1540
  79.5 5.8 %collective-permute-start.4 = (bf16[32,1024]{1,0:T(8,128)(2,1)S(1)}, bf16[32,1024]{1,0:T(8,128)(2,1)S(1)}, u32[]{:S(2)}, u32[]{:S(2)}) collective-permute-start(bf16[32,1024]{1,0:T(8,128)(2,1)S(1)} %get-tuple-element.15), channel_id=1, source_target_pairs={{0,4},{2,6},{4,0},{6,2},{1,5},{3,7},{5,1},{7,3},{8,12},{10,14},{12... | collective-permute-start | bytes 196616 | tf_op jit(solution)/shard_map/ppermute | solution.py:280
  81.4 5.5 %collective-permute-start.5 = (bf16[32,1024]{1,0:T(8,128)(2,1)S(1)}, bf16[32,1024]{1,0:T(8,128)(2,1)S(1)}, u32[]{:S(2)}, u32[]{:S(2)}) collective-permute-start(bf16[32,1024]{1,0:T(8,128)(2,1)S(1)} %get-tuple-element.16), channel_id=1, source_target_pairs={{0,6},{2,4},{4,2},{6,0},{1,7},{3,5},{5,3},{7,1},{8,14},{10,12},{12... | collective-permute-start | bytes 196616 | tf_op jit(solution)/shard_map/ppermute | solution.py:280
  83.5 4.3 %collective-permute-start.6 = (bf16[32,1024]{1,0:T(8,128)(2,1)S(1)}, bf16[32,1024]{1,0:T(8,128)(2,1)S(1)}, u32[]{:S(2)}, u32[]{:S(2)}) collective-permute-start(bf16[32,1024]{1,0:T(8,128)(2,1)S(1)} %get-tuple-element.17), channel_id=1, source_target_pairs={{0,2},{2,0},{4,6},{6,4},{1,3},{3,1},{5,7},{7,5},{8,10},{10,8},{12,... | collective-permute-start | bytes 196616 | tf_op jit(solution)/shard_map/ppermute | solution.py:280

commit v6 on v5

--- a/solution.py
+++ b/solution.py
@@ -61,10 +61,17 @@
                     loads_copy(c).wait()
                     phi_copy(c).wait()
                 cols = pl.multiple_of(tile * BLOCK, PAIR)
-                rows = jnp.concatenate([loads_ref[:, pl.ds(cols, BLOCK)], loads_ref[:, pl.ds(cols + BLOCK, BLOCK)]], axis=0)
-                both = jnp.concatenate([phi_ref[tile], phi_ref[tile + 1]], axis=1)
+                none = jnp.zeros((load_cols, BLOCK), BF16)
+                rows = jnp.concatenate(
+                    [
+                        jnp.concatenate([loads_ref[:, pl.ds(cols, BLOCK)], none], axis=1),
+                        jnp.concatenate([none, loads_ref[:, pl.ds(cols + BLOCK, BLOCK)]], axis=1),
+                    ],
+                    axis=0,
+                )
+                both = phi_ref[pl.ds(tile, 2)].reshape(PAIR, BLOCK)
                 terms = jnp.dot(rows, both, preferred_element_type=F32)
-                first, second = terms[:load_cols, :BLOCK], terms[load_cols:, BLOCK:]
+                first, second = terms[:load_cols], terms[load_cols:]
                 acc_ref[inc_ref[tile]] += jnp.where(tile < live, first, jnp.zeros_like(first))
                 acc_ref[inc_ref[tile + 1]] += jnp.where(tile + 1 < live, second, jnp.zeros_like(second))
             return carry
@@ -218,10 +225,13 @@
             owner, end, sens = carry
             for j in range(0, unroll, 2):
                 tile = p * unroll + j
-                rows = jnp.concatenate([block(tile), block(tile + 1)], axis=0)
-                both = phi_ref[pl.ds(tile, 2)].reshape(PAIR, BLOCK)
+                none = jnp.zeros((load_cols, BLOCK), BF16)
+                rows = jnp.concatenate(
+                    [jnp.concatenate([block(tile), none], axis=1), jnp.concatenate([none, block(tile + 1)], axis=1)], axis=0
+                )
+                both = jnp.concatenate([phi_ref[tile], phi_ref[tile + 1]], axis=1)
                 product = lax.dot_general(rows, both, contract, preferred_element_type=F32)
-                couplings = (product[:load_cols, :BLOCK], product[load_cols:, BLOCK:])
+                couplings = (product[:load_cols], product[load_cols:])
                 for q, coupling in enumerate(couplings):
                     past = (tile + q >= end) & (owner < subs)
                     owner = jnp.where(past, owner + 1, owner)

time: 109 us -> 109 us (level)
  no operation moved by 1% of the time
where the time goes in v6:
time: 109 us; the launch traced here: 108 us
  blocking collectives  76.7 us (70%)
  Pallas kernels  14 us (13%)
  starting transfers between devices  9.08 us (8%)
  waiting for transfers between devices  7.9 us (7%)
    all_to_all x4, blocking collectives, exchange(): return lax.all_to_all(parts, axis, 0, 0, tiled=True)  76.7 us
    ppermute x6, starting transfers between devices, swapped(): lax.ppermute(value, axis, [(i, i ^ bits) for i in range(lax.axis_size(axi...  8.99 us
    ppermute x6, waiting for transfers between devices, swapped(): lax.ppermute(value, axis, [(i, i ^ bits) for i in range(lax.axis_size(axi...  7.9 us
    pallas_call x1, Pallas kernels, condense(): pl.pallas_call(kernel, out_shape=(jax.ShapeDtypeStruct((peers, load_cols,...  4.78 us
    pallas_call x1, Pallas kernels, recover(): pl.pallas_call(kernel, out_shape=(jax.ShapeDtypeStruct(loads.shape, BF16)...  4.4 us
    pallas_call x1, Pallas kernels, times_transpose(): pl.pallas_call(kernel, out_shape=[jax.ShapeDtypeStruct((group, frows), BF...  2.32 us
  transfers between devices with their start and end apart: 7, of which 5 were waited for; matrix products, arithmetic and copies ran while one was open for 0% of the time, Pallas kernels for 5%

profile of v6, /device:TPU:0, one launch (start us, length us, event | category | flops | bytes accessed | tf_op | source)
XLA Modules:
  0.0 108.4 jit_solution(4045539078007762351)
XLA Ops:
  0.6 0.1 collective-permute-start.3
  0.7 0.0 copy-start
  0.7 4.8 %condense.1 = (bf16[16,32,1024]{2,1,0:T(8,128)(2,1)S(1)}, bf16[32,32768]{1,0:T(8,128)(2,1)S(1)}, bf16[256,128,128]{2,1,0:T(8,128)(2,1)S(1)}) custom-call(s32[256]{0:T(256)} %inc_hbm.3, s32[128]{0:T(128)} %sizes_hbm.3, bf16[32,32768]{1,0:T(8,128)(2,1)} %loads_hbm.1, bf16[256,128,128]{2,1,0:T(8,128)(2,1)} %phi_hbm.1), custom_call_target="tpu_custom_call" | custom-call | tf_op jit(solution)/shard_map/condense/pallas_call | solution.py:83
  5.5 24.8 %all_to_all.20.refs_0_ = bf16[16,32,1024]{2,1,0:T(8,128)(2,1)S(1)} all-to-all(bf16[16,32,1024]{2,1,0:T(8,128)(2,1)S(1)} %get-tuple-element.11), channel_id=1, replica_groups=mesh['x'=4,'y'=4,'z'=4,'c'=2] {'x','y'}, dimensions={0} | all-to-all | bytes 2097152 | tf_op jit(solution)/shard_map/all_to_all | solution.py:281
  30.3 0.1 total_of.3.after_ref.refs_0_
  30.5 4.0 %collective-permute-start.2 = (bf16[32,1024]{1,0:T(8,128)(2,1)S(1)}, bf16[32,1024]{1,0:T(8,128)(2,1)S(1)}, u32[]{:S(2)}, u32[]{:S(2)}) collective-permute-start(bf16[32,1024]{1,0:T(8,128)(2,1)S(1)} %total_of.3.after_ref.refs_0_), channel_id=1, source_target_pairs={{0,4},{2,6},{4,0},{6,2},{1,5},{3,7},{5,1},{7,3},{8,12},{10,14},{12... | collective-permute-start | bytes 196616 | tf_op jit(solution)/shard_map/ppermute | solution.py:290
  34.4 0.7 collective-permute-start.1
  35.1 0.3 collective-permute-start
  35.4 0.0 collective-permute-done.3.other_ref
  35.4 0.0 copy-done
  35.4 0.8 rounded.1
  36.3 0.5 collective-permute-done.2.refs_3_
  36.7 3.2 %collective-permute-done.1.refs_2_ = bf16[32,1024]{1,0:T(8,128)(2,1)S(1)} collective-permute-done((bf16[32,1024]{1,0:T(8,128)(2,1)S(1)}, bf16[32,1024]{1,0:T(8,128)(2,1)S(1)}, u32[]{:S(2)}, u32[]{:S(2)}) %collective-permute-start.1) | collective-permute-done | bytes 65568 | tf_op jit(solution)/shard_map/ppermute | solution.py:290
  39.9 0.0 collective-permute-done.refs_1_
  39.9 1.3 %times_factor.1 = bf16[128,4096]{1,0:T(8,128)(2,1)S(1)} custom-call(bf16[32,1024]{1,0:T(8,128)(2,1)S(1)} %total_of.3.after_ref.refs_0_, bf16[32,1024]{1,0:T(8,128)(2,1)S(1)} %collective-permute-done.refs_1_, bf16[32,1024]{1,0:T(8,128)(2,1)S(1)} %collective-permute-done.1.refs_2_, bf16[32,1024]{1,0:T(8,128)(2,1)S(1)} %collective-permute-done.2.refs_3_, ...), custom_call_target="tpu_custom_call" | custom-call | tf_op jit(solution)/shard_map/times_factor/pallas_call | solution.py:162
  41.2 18.5 %all_to_all.21.refs_0_ = bf16[16,8,4096]{2,1,0:T(8,128)(2,1)S(1)} all-to-all(bf16[16,8,4096]{2,1,0:T(8,128)(2,1)S(1)} %bitcast.4), channel_id=1, replica_groups=mesh['x'=4,'y'=4,'z'=4,'c'=2] {'x','y'}, dimensions={0} | all-to-all | bytes 2097152 | tf_op jit(solution)/shard_map/all_to_all | solution.py:281
  59.7 0.2 total_of.4
  59.8 17.3 %all_to_all.22 = bf16[16,8,4096]{2,1,0:T(8,128)(2,1)S(1)} all-to-all(bf16[16,8,4096]{2,1,0:T(8,128)(2,1)S(1)} %total_of.4), channel_id=1, replica_groups=mesh['x'=4,'y'=4,'z'=4,'c'=2] {'x','y'}, dimensions={0} | all-to-all | bytes 2097152 | tf_op jit(solution)/shard_map/all_to_all | solution.py:281
  77.1 0.0 copy-start.1
  77.1 0.0 copy-start.2
  77.1 0.0 copy-start.3
  77.1 0.0 copy-start.4
  77.1 2.3 %times_transpose.1 = (bf16[32,1024]{1,0:T(8,128)(2,1)S(1)}, bf16[32,1024]{1,0:T(8,128)(2,1)S(1)}, bf16[32,1024]{1,0:T(8,128)(2,1)S(1)}, bf16[32,1024]{1,0:T(8,128)(2,1)S(1)}) custom-call(bf16[128,4096]{1,0:T(8,128)(2,1)S(1)} %bitcast.3, bf16[1024,2048]{1,0:T(8,128)(2,1)S(1)} %get-tuple-element.12.refs_4_.own_ref, ...), custom_call_target="tpu_custom_call" | custom-call | tf_op jit(solution)/shard_map/times_transpose/pallas_call | solution.py:186
  79.5 2.0 %collective-permute-start.4 = (bf16[32,1024]{1,0:T(8,128)(2,1)S(1)}, bf16[32,1024]{1,0:T(8,128)(2,1)S(1)}, u32[]{:S(2)}, u32[]{:S(2)}) collective-permute-start(bf16[32,1024]{1,0:T(8,128)(2,1)S(1)} %get-tuple-element.15), channel_id=1, source_target_pairs={{0,4},{2,6},{4,0},{6,2},{1,5},{3,7},{5,1},{7,3},{8,12},{10,14},{12... | collective-permute-start | bytes 196616 | tf_op jit(solution)/shard_map/ppermute | solution.py:290
  81.4 2.1 %collective-permute-start.5 = (bf16[32,1024]{1,0:T(8,128)(2,1)S(1)}, bf16[32,1024]{1,0:T(8,128)(2,1)S(1)}, u32[]{:S(2)}, u32[]{:S(2)}) collective-permute-start(bf16[32,1024]{1,0:T(8,128)(2,1)S(1)} %get-tuple-element.16), channel_id=1, source_target_pairs={{0,6},{2,4},{4,2},{6,0},{1,7},{3,5},{5,3},{7,1},{8,14},{10,12},{12... | collective-permute-start | bytes 196616 | tf_op jit(solution)/shard_map/ppermute | solution.py:290
  83.5 0.0 collective-permute-start.6
  83.5 1.8 %collective-permute-done.4.refs_1_ = bf16[32,1024]{1,0:T(8,128)(2,1)S(1)} collective-permute-done((bf16[32,1024]{1,0:T(8,128)(2,1)S(1)}, bf16[32,1024]{1,0:T(8,128)(2,1)S(1)}, u32[]{:S(2)}, u32[]{:S(2)}) %collective-permute-start.4) | collective-permute-done | bytes 65568 | tf_op jit(solution)/shard_map/ppermute | solution.py:290
  85.3 1.6 %collective-permute-done.5.refs_2_ = bf16[32,1024]{1,0:T(8,128)(2,1)S(1)} collective-permute-done((bf16[32,1024]{1,0:T(8,128)(2,1)S(1)}, bf16[32,1024]{1,0:T(8,128)(2,1)S(1)}, u32[]{:S(2)}, u32[]{:S(2)}) %collective-permute-start.5) | collective-permute-done | bytes 65568 | tf_op jit(solution)/shard_map/ppermute | solution.py:290
  86.9 0.8 collective-permute-done.6.refs_3_
  87.7 0.1 total_of.5
  87.8 16.2 %all_to_all.23.amp_ref = bf16[16,32,1024]{2,1,0:T(8,128)(2,1)S(1)} all-to-all(bf16[16,32,1024]{2,1,0:T(8,128)(2,1)S(1)} %total_of.5), channel_id=1, replica_groups=mesh['x'=4,'y'=4,'z'=4,'c'=2] {'x','y'}, dimensions={0} | all-to-all | bytes 2097152 | tf_op jit(solution)/shard_map/all_to_all | solution.py:281
  104.0 0.0 copy-done.1
  104.0 0.0 copy-done.2
  104.0 0.0 copy-done.3
  104.0 0.0 copy-done.4
  104.0 4.4 %recover.1 = (bf16[32,32768]{1,0:T(8,128)(2,1)}, f32[32,128]{1,0:T(8,128)}) custom-call(s32[256]{0:T(256)S(1)} %copy-done.3, s32[128]{0:T(128)S(1)} %copy-done.4, bf16[16,32,1024]{2,1,0:T(8,128)(2,1)S(1)} %all_to_all.23.amp_ref, bf16[32,32768]{1,0:T(8,128)(2,1)S(1)} %get-tuple-element.18.loads_ref, bf16[32,32768]{1,0:T(8,128)(2,1)S(1)} %copy-done.1, ...), custom_call_target="tpu_custom_call" | custom-call | tf_op jit(solution)/shard_map/recover/pallas_call | solution.py:258
Async XLA Ops:
  0.6 34.8 %collective-permute-start.3 = (f32[1024,2048]{1,0:T(8,128)}, f32[1024,2048]{1,0:T(8,128)S(1)}, u32[]{:S(2)}, u32[]{:S(2)}) collective-permute-start(f32[1024,2048]{1,0:T(8,128)} %own_ref.1), channel_id=1, source_target_pairs={{0,1},{1,0},{2,3},{3,2},{4,5},{5,4},{6,7},{7,6},{8,9},{9,8},{10,11... | collective-permute-start | bytes 25165832 | tf_op jit(solution)/shard_map/ppermute | solution.py:286
  0.7 34.7 %copy-start = (f32[1024,2048]{1,0:T(8,128)S(1)}, f32[1024,2048]{1,0:T(8,128)}, u32[]{:S(2)}) copy-start(f32[1024,2048]{1,0:T(8,128)} %own_ref.1) | copy-start | bytes 25165828
  30.5 6.3 %collective-permute-start.2 = (bf16[32,1024]{1,0:T(8,128)(2,1)S(1)}, bf16[32,1024]{1,0:T(8,128)(2,1)S(1)}, u32[]{:S(2)}, u32[]{:S(2)}) collective-permute-start(bf16[32,1024]{1,0:T(8,128)(2,1)S(1)} %total_of.3.after_ref.refs_0_), channel_id=1, source_target_pairs={{0,4},{2,6},{4,0},{6,2},{1,5},{3,7},{5,1},{7,3},{8,12},{10,14},{12... | collective-permute-start | bytes 196616 | tf_op jit(solution)/shard_map/ppermute | solution.py:290
  34.4 5.5 %collective-permute-start.1 = (bf16[32,1024]{1,0:T(8,128)(2,1)S(1)}, bf16[32,1024]{1,0:T(8,128)(2,1)S(1)}, u32[]{:S(2)}, u32[]{:S(2)}) collective-permute-start(bf16[32,1024]{1,0:T(8,128)(2,1)S(1)} %total_of.3.after_ref.refs_0_), channel_id=1, source_target_pairs={{0,6},{2,4},{4,2},{6,0},{1,7},{3,5},{5,3},{7,1},{8,14},{10,12},{12... | collective-permute-start | bytes 196616 | tf_op jit(solution)/shard_map/ppermute | solution.py:290
  35.1 4.8 %collective-permute-start = (bf16[32,1024]{1,0:T(8,128)(2,1)S(1)}, bf16[32,1024]{1,0:T(8,128)(2,1)S(1)}, u32[]{:S(2)}, u32[]{:S(2)}) collective-permute-start(bf16[32,1024]{1,0:T(8,128)(2,1)S(1)} %total_of.3.after_ref.refs_0_), channel_id=1, source_target_pairs={{0,2},{2,0},{4,6},{6,4},{1,3},{3,1},{5,7},{7,5},{8,10},{10,8},{12,... | collective-permute-start | bytes 196616 | tf_op jit(solution)/shard_map/ppermute | solution.py:290
  77.1 26.9 %copy-start.1 = (bf16[32,32768]{1,0:T(8,128)(2,1)S(1)}, bf16[32,32768]{1,0:T(8,128)(2,1)}, u32[]{:S(2)}) copy-start(bf16[32,32768]{1,0:T(8,128)(2,1)} %state_ref.1) | copy-start | bytes 6291460
  77.1 26.9 %copy-start.2 = (f32[32768]{0:T(1024)S(1)}, f32[32768]{0:T(1024)}, u32[]{:S(2)}) copy-start(f32[32768]{0:T(1024)} %param.9) | copy-start | bytes 393220
  77.1 26.9 %copy-start.3 = (s32[256]{0:T(256)S(1)}, s32[256]{0:T(256)}, u32[]{:S(2)}) copy-start(s32[256]{0:T(256)} %inc_hbm.3) | copy-start | bytes 3076
  77.1 26.9 %copy-start.4 = (s32[128]{0:T(128)S(1)}, s32[128]{0:T(128)}, u32[]{:S(2)}) copy-start(s32[128]{0:T(128)} %sizes_hbm.3) | copy-start | bytes 1540
  79.5 5.8 %collective-permute-start.4 = (bf16[32,1024]{1,0:T(8,128)(2,1)S(1)}, bf16[32,1024]{1,0:T(8,128)(2,1)S(1)}, u32[]{:S(2)}, u32[]{:S(2)}) collective-permute-start(bf16[32,1024]{1,0:T(8,128)(2,1)S(1)} %get-tuple-element.15), channel_id=1, source_target_pairs={{0,4},{2,6},{4,0},{6,2},{1,5},{3,7},{5,1},{7,3},{8,12},{10,14},{12... | collective-permute-start | bytes 196616 | tf_op jit(solution)/shard_map/ppermute | solution.py:290
  81.4 5.5 %collective-permute-start.5 = (bf16[32,1024]{1,0:T(8,128)(2,1)S(1)}, bf16[32,1024]{1,0:T(8,128)(2,1)S(1)}, u32[]{:S(2)}, u32[]{:S(2)}) collective-permute-start(bf16[32,1024]{1,0:T(8,128)(2,1)S(1)} %get-tuple-element.16), channel_id=1, source_target_pairs={{0,6},{2,4},{4,2},{6,0},{1,7},{3,5},{5,3},{7,1},{8,14},{10,12},{12... | collective-permute-start | bytes 196616 | tf_op jit(solution)/shard_map/ppermute | solution.py:290
  83.5 4.3 %collective-permute-start.6 = (bf16[32,1024]{1,0:T(8,128)(2,1)S(1)}, bf16[32,1024]{1,0:T(8,128)(2,1)S(1)}, u32[]{:S(2)}, u32[]{:S(2)}) collective-permute-start(bf16[32,1024]{1,0:T(8,128)(2,1)S(1)} %get-tuple-element.17), channel_id=1, source_target_pairs={{0,2},{2,0},{4,6},{6,4},{1,3},{3,1},{5,7},{7,5},{8,10},{10,8},{12,... | collective-permute-start | bytes 196616 | tf_op jit(solution)/shard_map/ppermute | solution.py:290
